TPU v7x, 128 devices: a whole 4x4x4 slice. The times are simulated.
128 devices in a mesh: elem: 8 (over z, core), vox: 16 (over y, x).
Axes of the slice: x: 4, y: 4, z: 4, core: 2. Of those that a mesh axis runs over, the one named last changes fastest.
Arguments:
- echoes: bfloat16 [1024, 2, 64, 2048], P(('elem', 'vox')), may hold values from -12 to 12, as said below
- filter_taps: bfloat16 [2, 16], replicated, may hold values from -1.5 to 1.5
- visible: int32 [128, 128, 2], replicated, may hold values from -1 to 7, as said below
- window_start: int32 [2, 128, 128, 2], P(None, None, ('elem', 'vox')), may hold values from 0 to 384
- delays: int32 [2, 128, 128, 2, 1536], P(None, ('elem', 'vox')), may hold values from 0 to 507
- tile_gain: float32 [128], P(('elem', 'vox')), may hold values from 0.5 to 12, as said below
Outputs:
- doppler_power: float32 [128, 1536], P(('elem', 'vox'))
Inputs may be any that keep to these rules, and one draw needn't show every extreme that they name: `echoes`: echoes are blood signal plus a stronger tissue part that has few patterns over frames. `visible`: -1 marks an empty slot; the live entries of one tile and block are distinct; a tile has at most 192 live slots, some tile exactly 192, and in that tile one block fills all 2 of its slots. `tile_gain`: positive gains.
All inputs are finite; a program needn't handle non-finite values.
Results may differ from a plain program's by a relative error of at most 0.0004.
Values may be sent and summed in bfloat16 or wider, within the bound.
No kernel may reach another device: no remote copies, remote signals or barrier semaphores. Data moves between devices by JAX's collectives and lax.ppermute only.
A program may use at most 128 MiB of HBM per device.

v0:
```python
import jax
import jax.numpy as jnp
from jax import lax
from jax.sharding import PartitionSpec as P

W = 128


damping = 0.5


def project(windows, lag_block, weight_block):
    lag_vox = jnp.transpose(lag_block, (2, 1, 0))
    floor_row = lag_vox // 4
    fraction = (lag_vox - 4 * floor_row).astype(jnp.float32) * 0.25
    upper_weight = fraction * weight_block[None, :, None]
    lower_weight = (1.0 - fraction) * weight_block[None, :, None]
    position = lax.broadcasted_iota(jnp.int32, (1, 1, 1, windows.shape[2]), 3)
    weights = jnp.where(position == floor_row[..., None], lower_weight[..., None], 0.0)
    weights = weights + jnp.where(
        position == floor_row[..., None] + 1, upper_weight[..., None], 0.0
    )
    weights = weights.astype(jnp.bfloat16).reshape(lag_vox.shape[0], -1)
    return jnp.dot(
        weights, windows.reshape(-1, windows.shape[-1]), preferred_element_type=jnp.float32
    )


def shards(echoes, filter_taps, visible, window_start, delays, tile_gain):
    members, planes, frames, samples = echoes.shape
    decimated = samples // 4
    quarter = filter_taps.shape[1] // 4
    channels = 2 * frames
    grouped = jnp.pad(
        echoes.reshape(members, planes, frames, decimated, 4),
        ((0, 0), (0, 0), (0, 0), (0, quarter - 1), (0, 0)),
    )
    tap_table = filter_taps.reshape(2, quarter, 4)
    demod_sum = jnp.zeros((members, planes, decimated, 2, frames), jnp.float32)
    for tap_group in range(quarter):
        demod_sum = demod_sum + jnp.einsum(
            "epfnr,cr->epncf",
            grouped[:, :, :, tap_group : tap_group + decimated, :],
            tap_table[:, tap_group, :],
            preferred_element_type=jnp.float32,
        )
    baseband = demod_sum.reshape(members * planes * decimated, channels).astype(jnp.bfloat16)
    device_count = lax.axis_size("elem") * lax.axis_size("vox")
    my_index = lax.axis_index(("elem", "vox"))
    slot_count = visible.shape[1] * visible.shape[2]
    window_rows = W
    block_seen = lax.dynamic_index_in_dim(visible, my_index, 1, keepdims=False)
    block_live = block_seen >= 0
    element = jnp.maximum(block_seen, 0)
    starts = window_start[:, :, 0, :]
    plane_ids = jnp.arange(planes, dtype=jnp.int32)
    first_row = (element[None] * planes + plane_ids[:, None, None]) * decimated + starts
    row_ids = first_row[..., None] + jnp.arange(window_rows, dtype=jnp.int32)
    row_ids = jnp.transpose(row_ids, (1, 2, 0, 3))
    outgoing = jnp.take(baseband, row_ids, axis=0)
    outgoing = jnp.where(block_live[:, :, None, None, None], outgoing, jnp.zeros((), jnp.bfloat16))
    arrived = lax.all_to_all(outgoing, ("elem", "vox"), split_axis=0, concat_axis=0, tiled=True)
    arrived = arrived.reshape(slot_count, planes, window_rows, channels)
    voxels = delays.shape[-1]
    lag_table = delays.reshape(planes, slot_count, voxels)
    group_rows = 16
    source = arrived
    weight = jnp.ones((slot_count,), jnp.float32)

    def accumulate(turn_index, summed):
        first_slot = turn_index * group_rows
        windows = lax.dynamic_slice_in_dim(source, first_slot, group_rows, 0)
        lag_block = lax.dynamic_slice_in_dim(lag_table, first_slot, group_rows, 1)
        weight_block = lax.dynamic_slice_in_dim(weight, first_slot, group_rows, 0)
        return summed + project(windows, lag_block, weight_block)

    summed = lax.fori_loop(
        0, slot_count // group_rows, accumulate, jnp.zeros((voxels, channels), jnp.float32)
    )
    beamed = summed * tile_gain[0]
    local_gram = lax.dot_general(
        beamed, beamed, (((0,), (0,)), ((), ())), precision=lax.Precision.HIGHEST
    )
    frame_gram = lax.psum(local_gram, ("elem", "vox"))
    energy = jnp.trace(frame_gram)
    correlation = frame_gram * (channels / energy)
    identity = jnp.eye(channels, dtype=jnp.float32)
    factor = jnp.linalg.cholesky(correlation + damping * identity)
    half_solve = lax.linalg.triangular_solve(factor, damping * identity, left_side=True, lower=True)
    filter_matrix = lax.linalg.triangular_solve(
        factor, half_solve, left_side=True, lower=True, transpose_a=True
    )
    norm_scale = jnp.sqrt(energy / (channels * device_count * voxels))
    filtered = jnp.dot(beamed, filter_matrix, precision=lax.Precision.HIGHEST) / norm_scale
    log_power = jnp.log(jnp.mean(filtered * filtered, axis=-1) + 1e-06)
    return log_power.reshape(1, voxels)


def solution(mesh):
    placed = (
        P(("elem", "vox"), None, None, None),
        P(),
        P(),
        P(None, None, ("elem", "vox"), None),
        P(None, ("elem", "vox"), None, None, None),
        P(("elem", "vox")),
    )
    return jax.shard_map(
        shards, mesh=mesh, in_specs=placed, out_specs=P(("elem", "vox"), None), check_vma=False
    )
```

profile of v0, /device:TPU:0, one launch (start us, length us, event | category | flops | bytes accessed | tf_op | source)
XLA Modules:
  0.0 1239.6 jit_solution(7359187746829487161)
XLA Ops:
  6.5 0.9 copy-done
  9.5 10.0 copy.28
  19.5 12.8 %copy.29 = bf16[8,2,64,512,4]{3,4,2,1,0:T(4,128)(2,1)} copy(bf16[8,2,64,512,4]{2,0,4,3,1:T(8,128)(2,1)} %bitcast.92) | data formatting | bytes 8388608 | tf_op jit(solution)/shard_map/reshape | solution.py:35
  32.5 5.4 fusion.11
  37.9 4.7 fusion.13
  42.6 4.6 fusion.9
  47.2 6.5 fusion.8
  53.8 7.5 copy.40
  61.3 7.1 reshape.128
  68.6 227.3 %gather_fusion = bf16[65536,128]{1,0:T(8,128)(2,1)} fusion(bf16[8192,128]{1,0:T(8,128)(2,1)S(1)} %reshape.128, s32[65536]{0:T(1024)S(1)} %broadcast_clamp_fusion), kind=kCustom, calls=%fused_computation | custom fusion | bytes 33816576 | tf_op jit(solution)/shard_map/jit(_take)/gather | solution.py:60
  295.9 14.2 %select_select_fusion = bf16[128,2,2,128,128]{4,3,2,1,0:T(8,128)(2,1)} fusion(bf16[128,2,2,128,128]{4,3,2,1,0:T(8,128)(2,1)} %bitcast.91, pred[128,2,2,128]{3,2,1,0:T(4,128)(4,1)S(1)} %compare_and_fusion, pred[128,2]{1,0:T(8,128)(4,1)S(1)} %copy.26), kind=kLoop, calls=%fused_computation.20 | loop fusion | flops 16777216 | bytes 33620224 | tf_op jit(solution)/shard_map/jit(_where)/select_n | solution.py:61
  310.0 11.7 all-to-all-start
  321.8 4.3 copy.24
  326.7 221.1 %all-to-all-done = bf16[128,2,2,128,128]{4,3,2,1,0:T(8,128)(2,1)} async-done(((bf16[128,2,2,128,128]{4,3,2,1,0:T(8,128)(2,1)}), bf16[128,2,2,128,128]{4,3,2,1,0:T(8,128)(2,1)}, u32[]{:S(2)}, u32[]{:S(2)}) %all-to-all-start) | async-done | bytes 16777248 | tf_op jit(solution)/shard_map/all_to_all | solution.py:62
  547.9 492.8 %while.16 = (s32[]{:T(128)}, f32[1536,128]{1,0:T(8,128)}, s32[2,256,1536]{2,0,1:T(2,128)S(1)}, bf16[256,2,128,128]{3,2,1,0:T(8,128)(2,1)}, s32[]{:T(128)}, /*index=5*/s32[]{:T(128)}, s32[]{:T(128)}, s32[]{:T(128)}) while((s32[]{:T(128)}, f32[1536,128]{1,0:T(8,128)}, s32[2,256,1536]{2,0,1:T(2,128)S(1)}, ...), condition=%wide.region_1.2_spmd.clone, body=%wide.region_0.1_spmd.clone.sunk | while | flops 1649786880 | bytes 4587669 | solution.py:77
  547.9 1.3 broadcast_subtract_fusion.2
  549.2 0.8 broadcast_add_fusion.2
  549.9 28.6 %fusion.59 = f32[1536,128]{1,0:T(8,128)} fusion(f32[1536,16,2]{0,2,1:T(2,128)} %get-tuple-element.175, s32[1536,16,2]{0,2,1:T(2,128)} %broadcast_add_fusion.2, f32[1536,16,2]{0,2,1:T(2,128)} %get-tuple-element.177, s32[1536,16,2]{0,2,1:T(2,128)S(1)} %get-tuple-element.176, bf16[256,2,128,128]{3,2,1,0:T(8,128)(2,1)} %get-tuple-element.197, ...), kind=kOutput, calls=%fused_computation.6.clone.3 | convolution fusion | flops 1648754688 | bytes 3407877 | tf_op jit(solution)/shard_map/while/body/eval_jaxpr/dot_general | solution.py:24
  578.5 1.3 broadcast_subtract_fusion.2
  579.8 0.8 broadcast_add_fusion.2
  580.6 28.7 %fusion.59 = f32[1536,128]{1,0:T(8,128)} fusion(f32[1536,16,2]{0,2,1:T(2,128)} %get-tuple-element.175, s32[1536,16,2]{0,2,1:T(2,128)} %broadcast_add_fusion.2, f32[1536,16,2]{0,2,1:T(2,128)} %get-tuple-element.177, s32[1536,16,2]{0,2,1:T(2,128)S(1)} %get-tuple-element.176, bf16[256,2,128,128]{3,2,1,0:T(8,128)(2,1)} %get-tuple-element.197, ...), kind=kOutput, calls=%fused_computation.6.clone.3 | convolution fusion | flops 1648754688 | bytes 3407877 | tf_op jit(solution)/shard_map/while/body/eval_jaxpr/dot_general | solution.py:24
  609.3 1.3 broadcast_subtract_fusion.2
  610.6 0.8 broadcast_add_fusion.2
  611.4 28.7 %fusion.59 = f32[1536,128]{1,0:T(8,128)} fusion(f32[1536,16,2]{0,2,1:T(2,128)} %get-tuple-element.175, s32[1536,16,2]{0,2,1:T(2,128)} %broadcast_add_fusion.2, f32[1536,16,2]{0,2,1:T(2,128)} %get-tuple-element.177, s32[1536,16,2]{0,2,1:T(2,128)S(1)} %get-tuple-element.176, bf16[256,2,128,128]{3,2,1,0:T(8,128)(2,1)} %get-tuple-element.197, ...), kind=kOutput, calls=%fused_computation.6.clone.3 | convolution fusion | flops 1648754688 | bytes 3407877 | tf_op jit(solution)/shard_map/while/body/eval_jaxpr/dot_general | solution.py:24
  640.1 1.3 broadcast_subtract_fusion.2
  641.4 0.8 broadcast_add_fusion.2
  642.2 28.7 %fusion.59 = f32[1536,128]{1,0:T(8,128)} fusion(f32[1536,16,2]{0,2,1:T(2,128)} %get-tuple-element.175, s32[1536,16,2]{0,2,1:T(2,128)} %broadcast_add_fusion.2, f32[1536,16,2]{0,2,1:T(2,128)} %get-tuple-element.177, s32[1536,16,2]{0,2,1:T(2,128)S(1)} %get-tuple-element.176, bf16[256,2,128,128]{3,2,1,0:T(8,128)(2,1)} %get-tuple-element.197, ...), kind=kOutput, calls=%fused_computation.6.clone.3 | convolution fusion | flops 1648754688 | bytes 3407877 | tf_op jit(solution)/shard_map/while/body/eval_jaxpr/dot_general | solution.py:24
  670.9 1.3 broadcast_subtract_fusion.2
  672.2 0.8 broadcast_add_fusion.2
  673.0 28.7 %fusion.59 = f32[1536,128]{1,0:T(8,128)} fusion(f32[1536,16,2]{0,2,1:T(2,128)} %get-tuple-element.175, s32[1536,16,2]{0,2,1:T(2,128)} %broadcast_add_fusion.2, f32[1536,16,2]{0,2,1:T(2,128)} %get-tuple-element.177, s32[1536,16,2]{0,2,1:T(2,128)S(1)} %get-tuple-element.176, bf16[256,2,128,128]{3,2,1,0:T(8,128)(2,1)} %get-tuple-element.197, ...), kind=kOutput, calls=%fused_computation.6.clone.3 | convolution fusion | flops 1648754688 | bytes 3407877 | tf_op jit(solution)/shard_map/while/body/eval_jaxpr/dot_general | solution.py:24
  701.7 1.3 broadcast_subtract_fusion.2
  703.0 0.8 broadcast_add_fusion.2
  703.8 28.7 %fusion.59 = f32[1536,128]{1,0:T(8,128)} fusion(f32[1536,16,2]{0,2,1:T(2,128)} %get-tuple-element.175, s32[1536,16,2]{0,2,1:T(2,128)} %broadcast_add_fusion.2, f32[1536,16,2]{0,2,1:T(2,128)} %get-tuple-element.177, s32[1536,16,2]{0,2,1:T(2,128)S(1)} %get-tuple-element.176, bf16[256,2,128,128]{3,2,1,0:T(8,128)(2,1)} %get-tuple-element.197, ...), kind=kOutput, calls=%fused_computation.6.clone.3 | convolution fusion | flops 1648754688 | bytes 3407877 | tf_op jit(solution)/shard_map/while/body/eval_jaxpr/dot_general | solution.py:24
  732.5 1.3 broadcast_subtract_fusion.2
  733.8 0.8 broadcast_add_fusion.2
  734.6 28.7 %fusion.59 = f32[1536,128]{1,0:T(8,128)} fusion(f32[1536,16,2]{0,2,1:T(2,128)} %get-tuple-element.175, s32[1536,16,2]{0,2,1:T(2,128)} %broadcast_add_fusion.2, f32[1536,16,2]{0,2,1:T(2,128)} %get-tuple-element.177, s32[1536,16,2]{0,2,1:T(2,128)S(1)} %get-tuple-element.176, bf16[256,2,128,128]{3,2,1,0:T(8,128)(2,1)} %get-tuple-element.197, ...), kind=kOutput, calls=%fused_computation.6.clone.3 | convolution fusion | flops 1648754688 | bytes 3407877 | tf_op jit(solution)/shard_map/while/body/eval_jaxpr/dot_general | solution.py:24
  763.3 1.3 broadcast_subtract_fusion.2
  765.4 28.7 %fusion.59 = f32[1536,128]{1,0:T(8,128)} fusion(f32[1536,16,2]{0,2,1:T(2,128)} %get-tuple-element.175, s32[1536,16,2]{0,2,1:T(2,128)} %broadcast_add_fusion.2, f32[1536,16,2]{0,2,1:T(2,128)} %get-tuple-element.177, s32[1536,16,2]{0,2,1:T(2,128)S(1)} %get-tuple-element.176, bf16[256,2,128,128]{3,2,1,0:T(8,128)(2,1)} %get-tuple-element.197, ...), kind=kOutput, calls=%fused_computation.6.clone.3 | convolution fusion | flops 1648754688 | bytes 3407877 | tf_op jit(solution)/shard_map/while/body/eval_jaxpr/dot_general | solution.py:24
  794.1 1.3 broadcast_subtract_fusion.2
  795.4 0.8 broadcast_add_fusion.2
  796.2 28.7 %fusion.59 = f32[1536,128]{1,0:T(8,128)} fusion(f32[1536,16,2]{0,2,1:T(2,128)} %get-tuple-element.175, s32[1536,16,2]{0,2,1:T(2,128)} %broadcast_add_fusion.2, f32[1536,16,2]{0,2,1:T(2,128)} %get-tuple-element.177, s32[1536,16,2]{0,2,1:T(2,128)S(1)} %get-tuple-element.176, bf16[256,2,128,128]{3,2,1,0:T(8,128)(2,1)} %get-tuple-element.197, ...), kind=kOutput, calls=%fused_computation.6.clone.3 | convolution fusion | flops 1648754688 | bytes 3407877 | tf_op jit(solution)/shard_map/while/body/eval_jaxpr/dot_general | solution.py:24
  824.9 1.3 broadcast_subtract_fusion.2
  826.2 0.8 broadcast_add_fusion.2
  827.0 28.7 %fusion.59 = f32[1536,128]{1,0:T(8,128)} fusion(f32[1536,16,2]{0,2,1:T(2,128)} %get-tuple-element.175, s32[1536,16,2]{0,2,1:T(2,128)} %broadcast_add_fusion.2, f32[1536,16,2]{0,2,1:T(2,128)} %get-tuple-element.177, s32[1536,16,2]{0,2,1:T(2,128)S(1)} %get-tuple-element.176, bf16[256,2,128,128]{3,2,1,0:T(8,128)(2,1)} %get-tuple-element.197, ...), kind=kOutput, calls=%fused_computation.6.clone.3 | convolution fusion | flops 1648754688 | bytes 3407877 | tf_op jit(solution)/shard_map/while/body/eval_jaxpr/dot_general | solution.py:24
  855.7 1.3 broadcast_subtract_fusion.2
  857.8 28.7 %fusion.59 = f32[1536,128]{1,0:T(8,128)} fusion(f32[1536,16,2]{0,2,1:T(2,128)} %get-tuple-element.175, s32[1536,16,2]{0,2,1:T(2,128)} %broadcast_add_fusion.2, f32[1536,16,2]{0,2,1:T(2,128)} %get-tuple-element.177, s32[1536,16,2]{0,2,1:T(2,128)S(1)} %get-tuple-element.176, bf16[256,2,128,128]{3,2,1,0:T(8,128)(2,1)} %get-tuple-element.197, ...), kind=kOutput, calls=%fused_computation.6.clone.3 | convolution fusion | flops 1648754688 | bytes 3407877 | tf_op jit(solution)/shard_map/while/body/eval_jaxpr/dot_general | solution.py:24
  886.5 1.3 broadcast_subtract_fusion.2
  888.6 28.7 %fusion.59 = f32[1536,128]{1,0:T(8,128)} fusion(f32[1536,16,2]{0,2,1:T(2,128)} %get-tuple-element.175, s32[1536,16,2]{0,2,1:T(2,128)} %broadcast_add_fusion.2, f32[1536,16,2]{0,2,1:T(2,128)} %get-tuple-element.177, s32[1536,16,2]{0,2,1:T(2,128)S(1)} %get-tuple-element.176, bf16[256,2,128,128]{3,2,1,0:T(8,128)(2,1)} %get-tuple-element.197, ...), kind=kOutput, calls=%fused_computation.6.clone.3 | convolution fusion | flops 1648754688 | bytes 3407877 | tf_op jit(solution)/shard_map/while/body/eval_jaxpr/dot_general | solution.py:24
  917.3 1.3 broadcast_subtract_fusion.2
  919.4 28.7 %fusion.59 = f32[1536,128]{1,0:T(8,128)} fusion(f32[1536,16,2]{0,2,1:T(2,128)} %get-tuple-element.175, s32[1536,16,2]{0,2,1:T(2,128)} %broadcast_add_fusion.2, f32[1536,16,2]{0,2,1:T(2,128)} %get-tuple-element.177, s32[1536,16,2]{0,2,1:T(2,128)S(1)} %get-tuple-element.176, bf16[256,2,128,128]{3,2,1,0:T(8,128)(2,1)} %get-tuple-element.197, ...), kind=kOutput, calls=%fused_computation.6.clone.3 | convolution fusion | flops 1648754688 | bytes 3407877 | tf_op jit(solution)/shard_map/while/body/eval_jaxpr/dot_general | solution.py:24
  948.1 1.3 broadcast_subtract_fusion.2
  950.1 28.7 %fusion.59 = f32[1536,128]{1,0:T(8,128)} fusion(f32[1536,16,2]{0,2,1:T(2,128)} %get-tuple-element.175, s32[1536,16,2]{0,2,1:T(2,128)} %broadcast_add_fusion.2, f32[1536,16,2]{0,2,1:T(2,128)} %get-tuple-element.177, s32[1536,16,2]{0,2,1:T(2,128)S(1)} %get-tuple-element.176, bf16[256,2,128,128]{3,2,1,0:T(8,128)(2,1)} %get-tuple-element.197, ...), kind=kOutput, calls=%fused_computation.6.clone.3 | convolution fusion | flops 1648754688 | bytes 3407877 | tf_op jit(solution)/shard_map/while/body/eval_jaxpr/dot_general | solution.py:24
  978.9 1.3 broadcast_subtract_fusion.2
  980.9 28.7 %fusion.59 = f32[1536,128]{1,0:T(8,128)} fusion(f32[1536,16,2]{0,2,1:T(2,128)} %get-tuple-element.175, s32[1536,16,2]{0,2,1:T(2,128)} %broadcast_add_fusion.2, f32[1536,16,2]{0,2,1:T(2,128)} %get-tuple-element.177, s32[1536,16,2]{0,2,1:T(2,128)S(1)} %get-tuple-element.176, bf16[256,2,128,128]{3,2,1,0:T(8,128)(2,1)} %get-tuple-element.197, ...), kind=kOutput, calls=%fused_computation.6.clone.3 | convolution fusion | flops 1648754688 | bytes 3407877 | tf_op jit(solution)/shard_map/while/body/eval_jaxpr/dot_general | solution.py:24
  1009.7 1.3 broadcast_subtract_fusion.2
  1011.7 28.7 %fusion.59 = f32[1536,128]{1,0:T(8,128)} fusion(f32[1536,16,2]{0,2,1:T(2,128)} %get-tuple-element.175, s32[1536,16,2]{0,2,1:T(2,128)} %broadcast_add_fusion.2, f32[1536,16,2]{0,2,1:T(2,128)} %get-tuple-element.177, s32[1536,16,2]{0,2,1:T(2,128)S(1)} %get-tuple-element.176, bf16[256,2,128,128]{3,2,1,0:T(8,128)(2,1)} %get-tuple-element.197, ...), kind=kOutput, calls=%fused_computation.6.clone.3 | convolution fusion | flops 1648754688 | bytes 3407877 | tf_op jit(solution)/shard_map/while/body/eval_jaxpr/dot_general | solution.py:24
  1040.6 3.4 fusion.21
  1044.1 157.6 %all-reduce.3.cloned.1.call-done = f32[128,128]{1,0:T(8,128)} async-done(((f32[128,128]{1,0:T(8,128)}), f32[128,128]{1,0:T(8,128)}) %all-reduce.3.cloned.1.call-update) | async-done | bytes 65552 | tf_op jit(solution)/shard_map/psum | solution.py:84
  1201.7 1.5 select_reduce_fusion.1
  1203.9 0.9 select_add_fusion
  1204.8 0.9 fusion.31
  1205.7 11.7 cholesky.18
  1218.9 9.8 custom-call.8
  1229.9 2.0 fusion.19
  (37 shorter events, 10.3 us)
Async XLA Ops:
  6.5 0.9 copy-start
  19.5 12.8 %copy-start.3 = (bf16[2,16]{1,0:T(2,128)(2,1)S(1)}, bf16[2,16]{1,0:T(2,128)(2,1)}, u32[]{:S(2)}) copy-start(bf16[2,16]{1,0:T(2,128)(2,1)} %param.9) | copy-start | bytes 196
  32.5 5.5 copy-start.2
  310.0 237.8 %all-to-all-start = ((bf16[128,2,2,128,128]{4,3,2,1,0:T(8,128)(2,1)}), bf16[128,2,2,128,128]{4,3,2,1,0:T(8,128)(2,1)}, u32[]{:S(2)}, u32[]{:S(2)}) async-start(bf16[128,2,2,128,128]{4,3,2,1,0:T(8,128)(2,1)} %select_select_fusion), calls=%async_computation | async-start | bytes 33554432 | tf_op jit(solution)/shard_map/all_to_all | solution.py:62
  321.7 880.0 %all-reduce.3.cloned.1.call-start = ((), (), s32[]{:S(2)}) async-start(), calls=%async_computation.1 | async-start | bytes 131072 | tf_op jit(solution)/shard_map/psum | solution.py:84
  1040.6 191.9 %copy-start.1 = (s32[128,128,2]{1,2,0:T(2,128)S(1)}, s32[128,128,2]{1,2,0:T(2,128)}, u32[]{:S(2)}) copy-start(s32[128,128,2]{1,2,0:T(2,128)} %param.10) | copy-start | bytes 393220
Sparse Core Ops, SparseCore 0:
  1044.2 157.4 all-reduce.2
where the time goes:
time: 1260 us; the launch traced here: 1240 us
  matrix products  487 us (39%)
  waiting for transfers between devices  379 us (30%)
  local copies, waits for them, and re-layouts  271 us (22%)
  other arithmetic  74.9 us (6%)
  between operations  15.8 us (1%)
    dot_general x16, matrix products, project(): jnp.dot(weights, windows.reshape(-1, windows.shape[-1]), preferred_elemen...  460 us
    gather x1, local copies, waits for them, and re-layouts, shards(): outgoing = jnp.take(baseband, row_ids, axis=0)  227 us
    all_to_all x1, waiting for transfers between devices, shards(): lax.all_to_all(outgoing, ('elem', 'vox'), split_axis=0, concat_axis=0, ti...  221 us
    psum x1, waiting for transfers between devices, shards(): frame_gram = lax.psum(local_gram, ('elem', 'vox'))  158 us
  transfers between devices with their start and end apart: 2, of which 2 were waited for; matrix products, arithmetic and copies ran while one was open for 0% of the time, Pallas kernels for 0%

commit v1 on v0

v1 whole, which is shorter than its diff:
```python
import jax
import jax.numpy as jnp
from jax import lax
from jax.experimental import pallas as pl
from jax.experimental.pallas import tpu as pltpu
from jax.sharding import PartitionSpec as P

W = 128
damping = 0.5
AXES = ("elem", "vox")
BF, F32 = jnp.bfloat16, jnp.float32

FIRST = ((0, 0), (0, 1), (1, 0))
SECOND = ((1, 1),)
TILES_PER_STEP = 8


def window_kernel(elem_ref, start_ref, band_ref, echo_ref, first_ref, second_ref, base_ref):
    step = pl.program_id(0)
    members = base_ref.shape[0]

    @pl.when(step < members)
    def _():
        rows = []
        for plane in range(2):
            x = echo_ref[0, plane]
            x = jnp.concatenate([x, jnp.zeros((x.shape[0], 128), x.dtype)], axis=1)
            for j in range(4):
                rows.append(x[:, 512 * j : 512 * j + 640])
        out = jnp.dot(jnp.concatenate(rows, axis=0), band_ref[...], preferred_element_type=F32)
        out = out.astype(BF).astype(F32)
        for plane in range(2):
            for j in range(4):
                r = 64 * (4 * plane + j)
                base_ref[step, plane, j, 0:64, :] = out[r : r + 64, 0:128]
                base_ref[step, plane, j, 64:128, :] = out[r : r + 64, 128:256]

    @pl.when(step >= members)
    def _():
        lane = lax.broadcasted_iota(jnp.int32, (128, 128), 1)

        def one_tile(i, carry):
            tile = (step - members) * TILES_PER_STEP + i
            for ref, units in ((first_ref, FIRST), (second_ref, SECOND)):
                for k, (slot, plane) in enumerate(units):
                    seen = elem_ref[tile * 2 + slot]
                    member = jnp.maximum(seen, 0)
                    start = start_ref[(plane * 128 + tile) * 2 + slot]
                    block = start // 128
                    shift = start - 128 * block
                    here = base_ref[member, plane, block]
                    after = base_ref[member, plane, jnp.minimum(block + 1, 3)]
                    both = jnp.where(lane >= shift, here, after)
                    out = pltpu.roll(both, (128 - shift) & 127, 1)
                    out = jnp.where(seen >= 0, out, 0.0)
                    ref[i, k] = out.astype(BF)
            return carry

        lax.fori_loop(0, TILES_PER_STEP, one_tile, 0)


def make_windows(echoes, band, seen, starts):
    members, planes, frames, samples = echoes.shape
    tiles = seen.shape[0] // 2
    steps = members + tiles // TILES_PER_STEP
    last = members - 1

    def out_map(i, *_):
        return (jnp.maximum(i - members, 0), 0, 0, 0)

    return pl.pallas_call(
        window_kernel,
        grid_spec=pltpu.PrefetchScalarGridSpec(
            num_scalar_prefetch=2,
            grid=(steps,),
            in_specs=[
                pl.BlockSpec(band.shape, lambda i, *_: (0, 0)),
                pl.BlockSpec((1, planes, frames, samples), lambda i, *_: (jnp.minimum(i, last), 0, 0, 0)),
            ],
            out_specs=[
                pl.BlockSpec((TILES_PER_STEP, len(FIRST), 128, 128), out_map),
                pl.BlockSpec((TILES_PER_STEP, len(SECOND), 128, 128), out_map),
            ],
            scratch_shapes=[pltpu.VMEM((members, planes, 4, 128, 128), F32)],
        ),
        out_shape=[
            jax.ShapeDtypeStruct((tiles, len(FIRST), 128, 128), BF),
            jax.ShapeDtypeStruct((tiles, len(SECOND), 128, 128), BF),
        ],
        compiler_params=pltpu.CompilerParams(vmem_limit_bytes=48 * 2**20),
        cost_estimate=pl.CostEstimate(flops=2 * 10**9, bytes_accessed=24 * 2**20, transcendentals=0),
        name="windows",
    )(seen, starts, band, echoes)


def build_weights(out_ref, row, lag):
    lag = jnp.broadcast_to(lag.astype(F32) * 0.25 - 64.0, (16, lag.shape[1])).astype(BF)
    iota = lax.broadcasted_iota(jnp.int32, (16, 128), 0).astype(F32)
    rows = [(iota + (16.0 * w - 64.0)).astype(BF) for w in range(8)]
    one, zero = jnp.ones((), BF), jnp.zeros((), BF)
    for c in range(lag.shape[1] // 128):
        d = lag[:, 128 * c : 128 * c + 128]
        for w in range(8):
            out_ref[row + 16 * w : row + 16 * w + 16, 128 * c : 128 * c + 128] = jnp.maximum(
                one - jnp.abs(d - rows[w]), zero
            )


def accumulate(units, group, chunk, windows_ref, lag_ref, acc_ref, weight_ref):
    todo = [(b, k) for b in range(group) for k in range(len(units))]
    for n, at in enumerate(range(0, len(todo), chunk)):
        part = todo[at : at + chunk]
        half = weight_ref.at[n % 2]
        for m, (b, k) in enumerate(part):
            slot, plane = units[k]
            build_weights(half, 128 * m, lag_ref[plane, b, slot : slot + 1, :])
        lhs = jnp.concatenate([windows_ref[b, k] for b, k in part], axis=1)
        acc_ref[...] += jnp.dot(lhs, half[...], preferred_element_type=F32)


def first_beam_kernel(units, group, chunk, lag_ref, windows_ref, out_ref, weight_ref):
    @pl.when(pl.program_id(0) == 0)
    def _():
        out_ref[...] = jnp.zeros_like(out_ref)

    accumulate(units, group, chunk, windows_ref, lag_ref, out_ref, weight_ref)


def second_beam_kernel(units, group, chunk, gain_ref, lag_ref, windows_ref, before_ref, out_ref, gram_ref, weight_ref):
    @pl.when(pl.program_id(0) == 0)
    def _():
        out_ref[...] = before_ref[...]

    accumulate(units, group, chunk, windows_ref, lag_ref, out_ref, weight_ref)

    @pl.when(pl.program_id(0) == pl.num_programs(0) - 1)
    def _():
        beam = out_ref[...] * gain_ref[0]
        out_ref[...] = beam
        gram_ref[...] = lax.dot_general(
            beam, beam, (((1,), (1,)), ((), ())), precision=lax.Precision.HIGHEST, preferred_element_type=F32
        )


def beam_call(units, group, chunk, lags, windows, gain=None, before=None):
    planes, blocks, slots, voxels = lags.shape
    body = second_beam_kernel if before is not None else first_beam_kernel
    in_specs = [
        pl.BlockSpec((planes, group, slots, voxels), lambda i: (0, i, 0, 0)),
        pl.BlockSpec((group, len(units), 128, 128), lambda i: (i, 0, 0, 0)),
    ]
    args = [lags, windows]
    whole = pl.BlockSpec((128, voxels), lambda i: (0, 0))
    out_shape = [jax.ShapeDtypeStruct((128, voxels), F32)]
    out_specs = [whole]
    if before is not None:
        in_specs = [pl.BlockSpec(memory_space=pltpu.SMEM)] + in_specs + [whole]
        args = [gain] + args + [before]
        out_shape.append(jax.ShapeDtypeStruct((128, 128), F32))
        out_specs.append(pl.BlockSpec((128, 128), lambda i: (0, 0)))

    def kernel(*refs):
        body(units, group, chunk, *refs)

    return pl.pallas_call(
        kernel,
        grid=(blocks // group,),
        in_specs=in_specs,
        out_specs=out_specs,
        out_shape=out_shape,
        scratch_shapes=[pltpu.VMEM((2, 128 * chunk, voxels), BF)],
        compiler_params=pltpu.CompilerParams(vmem_limit_bytes=48 * 2**20),
        cost_estimate=pl.CostEstimate(
            flops=2 * 128 * voxels * 128 * blocks * len(units),
            bytes_accessed=blocks * len(units) * (128 * 256 + 8 * voxels),
            transcendentals=0,
        ),
        name="beam",
    )(*args)


def exchange_sum(x):
    for axis, digits in (("elem", (1,)), ("elem", (2, 4, 6)), ("vox", (1, 2, 3)), ("vox", (4, 8, 12))):
        size = lax.axis_size(axis)
        parts = [lax.ppermute(x, axis, [(i, i ^ k) for i in range(size)]) for k in digits]
        for part in parts:
            x = x + part
    return x


def shards(echoes, filter_taps, visible, window_start, delays, tile_gain):
    members, planes, frames, samples = echoes.shape
    channels = 2 * frames
    device_count = lax.axis_size("elem") * lax.axis_size("vox")
    voxels = delays.shape[-1]
    my_index = lax.axis_index(AXES)

    offset = (
        lax.broadcasted_iota(jnp.int32, (640, 2, 128), 0) - 4 * lax.broadcasted_iota(jnp.int32, (640, 2, 128), 2)
    )
    band = jnp.zeros((640, 2, 128), BF)
    for k in range(filter_taps.shape[1]):
        band = jnp.where(offset == k, filter_taps[None, :, k : k + 1], band)
    band = band.reshape(640, 256)

    seen = lax.dynamic_index_in_dim(visible, my_index, 1, keepdims=False).reshape(-1)
    starts = window_start[:, :, 0, :].reshape(-1)
    first, second = make_windows(echoes, band, seen, starts)

    first = lax.all_to_all(first, AXES, split_axis=0, concat_axis=0, tiled=True)
    second = lax.all_to_all(second, AXES, split_axis=0, concat_axis=0, tiled=True)
    lags = delays[:, 0]
    (partial,) = beam_call(FIRST, 4, 4, lags, first)
    beam, local_gram = beam_call(SECOND, 8, 4, lags, second, tile_gain, partial)

    frame_gram = exchange_sum(local_gram)
    energy = jnp.trace(frame_gram)
    correlation = frame_gram * (channels / energy)
    identity = jnp.eye(channels, dtype=F32)
    factor = jnp.linalg.cholesky(correlation + damping * identity)
    half_solve = lax.linalg.triangular_solve(factor, damping * identity, left_side=True, lower=True)
    filter_matrix = lax.linalg.triangular_solve(
        factor, half_solve, left_side=True, lower=True, transpose_a=True
    )
    norm_scale = jnp.sqrt(energy / (channels * device_count * voxels))
    filtered = jnp.dot(filter_matrix, beam, precision=lax.Precision.HIGHEST) / norm_scale
    log_power = jnp.log(jnp.mean(filtered * filtered, axis=0) + 1e-06)
    return log_power.reshape(1, voxels)


def solution(mesh):
    placed = (
        P(AXES, None, None, None),
        P(),
        P(),
        P(None, None, AXES, None),
        P(None, AXES, None, None, None),
        P(AXES),
    )
    return jax.shard_map(
        shards, mesh=mesh, in_specs=placed, out_specs=P(AXES, None), check_vma=False
    )
```

time: 1260 us -> 342 us (0.27); the launches traced: 1240 us -> 342 us
  matrix products: 487 us -> 2.42 us
  waiting for transfers between devices: 379 us -> 16.3 us
  local copies, waits for them, and re-layouts: 271 us -> 9.32 us
  blocking collectives: 0 us -> 152 us
  Pallas kernels: 0 us -> 114 us
  other arithmetic: 74.9 us -> 24.4 us
  between operations: 15.8 us -> 2.22 us
    dot_general x22 -> x1, matrix products: 486 us -> 1.93 us  [shards(): jnp.dot(filter_matrix, beam, precision=lax.Precision.HIGHEST) / norm_scale]
    gather x1 -> x0, local copies, waits for them, and re-layouts: 227 us -> none  [shards(): outgoing = jnp.take(baseband, row_ids, axis=0)]
    all_to_all x1, waiting for transfers between devices: 221 us -> 0.01 us  [shards(): lax.all_to_all(second, AXES, split_axis=0, concat_axis=0, tiled=True)]
    psum x1 -> x0, waiting for transfers between devices: 158 us -> none  [shards(): frame_gram = lax.psum(local_gram, ('elem', 'vox'))]
    all_to_all x0 -> x1, blocking collectives: none -> 152 us  [shards(): first = lax.all_to_all(first, AXES, split_axis=0, concat_axis=0, tiled=True)]
    pallas_call x0 -> x3, Pallas kernels: none -> 114 us  [the longest x2 90.4 us: beam_call(): pl.pallas_call(kernel, grid=(blocks // group,), in_specs=in_specs, out_sp...]
    sub x16 -> x0, other arithmetic: 20.9 us -> none  [project(): lower_weight = (1.0 - fraction) * weight_block[None, :, None]]
    ppermute x0 -> x10, waiting for transfers between devices: none -> 16.3 us  [exchange_sum(): lax.ppermute(x, axis, [(i, i ^ k) for i in range(size)])]
  transfers between devices with their start and end apart: 2 -> 11, of which waited for: 2 -> 7; matrix products, arithmetic and copies ran while one was open for 0% -> 0% of each run, Pallas kernels for 0% -> 19%
where the time goes in v1:
time: 342 us
  blocking collectives  152 us (44%)
  Pallas kernels  114 us (33%)
  other arithmetic  24.4 us (7%)
  starting transfers between devices  20.8 us (6%)
  waiting for transfers between devices  16.3 us (5%)
  local copies, waits for them, and re-layouts  9.32 us (3%)
    all_to_all x1, blocking collectives, shards(): first = lax.all_to_all(first, AXES, split_axis=0, concat_axis=0, tiled=True)  152 us
    pallas_call x2, Pallas kernels, beam_call(): pl.pallas_call(kernel, grid=(blocks // group,), in_specs=in_specs, out_sp...  90.4 us
    pallas_call x1, Pallas kernels, make_windows(): pl.pallas_call(window_kernel, grid_spec=pltpu.PrefetchScalarGridSpec(num_...  23.9 us
    ppermute x10, waiting for transfers between devices, exchange_sum(): lax.ppermute(x, axis, [(i, i ^ k) for i in range(size)])  16.3 us
    ppermute x10, starting transfers between devices, exchange_sum(): lax.ppermute(x, axis, [(i, i ^ k) for i in range(size)])  14.3 us
    another operation x3, other arithmetic, shards(): factor = jnp.linalg.cholesky(correlation + damping * identity)  12.5 us
    another operation x2, other arithmetic, shards(): lax.linalg.triangular_solve(factor, half_solve, left_side=True, lower=Tru...  10.4 us
  transfers between devices with their start and end apart: 11, of which 7 were waited for; matrix products, arithmetic and copies ran while one was open for 0% of the time, Pallas kernels for 19%

profile of v1, /device:TPU:0, one launch (start us, length us, event | category | flops | bytes accessed | tf_op | source)
XLA Modules:
  0.0 342.0 jit_solution(7835998980446131517)
XLA Ops:
  0.0 0.0 copy-start
  0.0 1.7 slice_reduce_fusion.15
  1.7 0.0 copy-done
  1.7 2.4 dynamic-slice_reduce_fusion
  4.1 0.1 reshape.69.elem_ref
  4.2 0.8 copy.8
  5.1 0.1 reshape_squeeze.3.start_ref
  5.2 0.1 broadcast_bitcast_fusion.1
  5.3 0.1 broadcast_bitcast_fusion.3
  5.4 0.1 broadcast_bitcast_fusion.5
  5.4 0.1 broadcast_bitcast_fusion.7
  5.5 0.1 broadcast_bitcast_fusion.9
  5.6 0.1 broadcast_bitcast_fusion.11
  5.7 0.1 broadcast_bitcast_fusion.13
  5.7 0.1 broadcast_bitcast_fusion.15
  5.8 0.7 fusion.18.band_ref
  6.6 23.9 %windows.1 = (bf16[128,3,128,128]{3,2,1,0:T(8,128)(2,1)}, bf16[128,1,128,128]{3,2,1,0:T(8,128)(2,1)S(1)}) custom-call(s32[256]{0:T(256)S(1)} %reshape.69.elem_ref, s32[512]{0:T(512)S(1)} %reshape_squeeze.3.start_ref, bf16[640,256]{1,0:T(8,128)(2,1)S(1)} %fusion.18.band_ref, bf16[8,2,64,2048]{3,2,1,0:T(8,128)(2,1)} %echo_ref.1), custom_call_target="tpu_custom_call" | custom-call | flops 2000000000 | bytes 25165824 | tf_op jit(solution)/shard_map/windows/pallas_call | solution.py:71
  30.5 0.0 copy-start.1
  30.5 152.2 %all_to_all.10.refs_1_ = bf16[128,3,128,128]{3,2,1,0:T(8,128)(2,1)} all-to-all(bf16[128,3,128,128]{3,2,1,0:T(8,128)(2,1)} %get-tuple-element.10), channel_id=1, replica_groups=mesh['elem'=8,'vox'=16] {'elem','vox'}, dimensions={0} | all-to-all | bytes 25165824 | tf_op jit(solution)/shard_map/all_to_all | solution.py:210
  182.7 0.0 copy-done.1
  182.7 0.0 copy-start.2
  182.7 6.4 %all-to-all-start = ((bf16[128,1,128,128]{3,2,1,0:T(8,128)(2,1)}), bf16[128,1,128,128]{3,2,1,0:T(8,128)(2,1)}, u32[]{:S(2)}, u32[]{:S(2)}) async-start(bf16[128,1,128,128]{3,2,1,0:T(8,128)(2,1)} %copy-done.1), calls=%async_computation | async-start | bytes 8388608 | tf_op jit(solution)/shard_map/all_to_all | solution.py:211
  189.8 0.0 copy-done.2
  189.8 66.4 %beam.2.refs_3_ = f32[128,1536]{1,0:T(8,128)S(1)} custom-call(s32[2,128,2,1536]{3,2,1,0:T(2,128)S(1)} %bitcast.53, bf16[128,3,128,128]{3,2,1,0:T(8,128)(2,1)} %all_to_all.10.refs_1_), custom_call_target="tpu_custom_call" | custom-call | flops 19327352832 | bytes 17301504 | tf_op jit(solution)/shard_map/beam/pallas_call | solution.py:165
  256.2 0.0 copy-start.4
  256.2 0.9 copy-done.4
  257.1 0.0 all-to-all-done.refs_2_
  257.1 0.0 copy-start.5
  257.1 1.1 copy-done.5
  258.2 24.0 %beam.3 = (f32[128,1536]{1,0:T(8,128)S(1)}, f32[128,128]{1,0:T(8,128)S(1)}) custom-call(f32[1]{0:T(128)S(6)} %copy.10.refs_0_, s32[2,128,2,1536]{3,2,1,0:T(2,128)S(1)} %bitcast.54, bf16[128,1,128,128]{3,2,1,0:T(8,128)(2,1)} %all-to-all-done.refs_2_, f32[128,1536]{1,0:T(8,128)S(1)} %copy-done.5), custom_call_target="tpu_custom_call" | custom-call | flops 6442450944 | bytes 5767168 | tf_op jit(solution)/shard_map/beam/pallas_call | solution.py:165
  282.2 0.0 copy-start.3
  282.3 0.9 copy-done.3
  283.1 0.0 collective-permute-start
  283.1 1.3 collective-permute-done
  284.4 1.1 collective-permute-start.1
  285.5 3.2 collective-permute-start.2
  288.7 0.5 collective-permute-start.3
  289.2 0.0 collective-permute-done.1
  289.2 3.1 collective-permute-done.2
  292.2 1.9 collective-permute-done.3
  294.2 1.6 collective-permute-start.4
  295.7 2.7 collective-permute-start.5
  298.5 0.5 collective-permute-start.6
  299.0 0.0 collective-permute-done.4
  299.0 2.7 collective-permute-done.5
  301.6 2.3 collective-permute-done.6
  304.0 1.6 collective-permute-start.7
  305.6 2.8 collective-permute-start.8
  308.4 0.4 collective-permute-start.9
  308.7 0.0 collective-permute-done.7
  308.7 2.6 collective-permute-done.8
  311.3 2.5 collective-permute-done.9
  313.8 0.6 select_reduce_fusion.1
  315.2 0.1 copy.9
  315.3 11.7 %cholesky.18 = f32[128,128]{1,0:T(8,128)S(1)} custom-call(f32[128,128]{1,0:T(8,128)S(1)} %fusion.40), custom_call_target="Cholesky" | custom-call | tf_op jit(solution)/shard_map/jit(cholesky)/cholesky | solution.py:220
  327.1 0.7 compare_reduce_fusion
  327.8 0.6 fusion.36
  328.4 9.8 %custom-call.8 = f32[1,128,128]{1,2,0:T(8,128)S(1)} custom-call(f32[1,128,128]{2,1,0:T(8,128)S(1)} %fusion.36), custom_call_target="InvertDiagBlocksLowerTriangular" | custom-call | tf_op jit(solution)/shard_map/triangular_solve | solution.py:222
  338.2 0.3 fusion.34
  338.5 0.2 fusion.37
  339.4 1.9 fusion.1
  341.4 0.6 log.14
  (9 shorter events, 0.1 us)
Async XLA Ops:
  0.0 1.7 copy-start
  30.5 152.2 %copy-start.1 = (bf16[128,1,128,128]{3,2,1,0:T(8,128)(2,1)}, bf16[128,1,128,128]{3,2,1,0:T(8,128)(2,1)S(1)}, u32[]{:S(2)}) copy-start(bf16[128,1,128,128]{3,2,1,0:T(8,128)(2,1)S(1)} %get-tuple-element.9) | copy-start | bytes 12582916
  182.7 7.1 %copy-start.2 = (s32[2,1,128,2,1536]{4,3,2,1,0:T(2,128)S(1)}, s32[2,1,128,2,1536]{4,3,2,1,0:T(2,128)}, u32[]{:S(2)}) copy-start(s32[2,1,128,2,1536]{4,3,2,1,0:T(2,128)} %param.10) | copy-start | bytes 9437188
  182.7 74.4 %all-to-all-start = ((bf16[128,1,128,128]{3,2,1,0:T(8,128)(2,1)}), bf16[128,1,128,128]{3,2,1,0:T(8,128)(2,1)}, u32[]{:S(2)}, u32[]{:S(2)}) async-start(bf16[128,1,128,128]{3,2,1,0:T(8,128)(2,1)} %copy-done.1), calls=%async_computation | async-start | bytes 8388608 | tf_op jit(solution)/shard_map/all_to_all | solution.py:211
  256.2 0.9 copy-start.4
  257.1 1.1 copy-start.5
  282.2 0.9 copy-start.3
  283.1 1.3 collective-permute-start
  284.4 4.8 %collective-permute-start.1 = (f32[128,128]{1,0:T(8,128)S(1)}, f32[128,128]{1,0:T(8,128)S(1)}, u32[]{:S(2)}, u32[]{:S(2)}) collective-permute-start(f32[128,128]{1,0:T(8,128)S(1)} %add.69), channel_id=1, source_target_pairs={{0,32},{16,48},{32,0},{48,16},{64,96},{80,112},{96,64},{112,80},{1... | collective-permute-start | bytes 196616 | tf_op jit(solution)/shard_map/ppermute | solution.py:185
  285.5 6.8 %collective-permute-start.2 = (f32[128,128]{1,0:T(8,128)S(1)}, f32[128,128]{1,0:T(8,128)S(1)}, u32[]{:S(2)}, u32[]{:S(2)}) collective-permute-start(f32[128,128]{1,0:T(8,128)S(1)} %add.69), channel_id=1, source_target_pairs={{0,64},{16,80},{32,96},{48,112},{64,0},{80,16},{96,32},{112,48},{1... | collective-permute-start | bytes 196616 | tf_op jit(solution)/shard_map/ppermute | solution.py:185
  288.7 5.5 %collective-permute-start.3 = (f32[128,128]{1,0:T(8,128)S(1)}, f32[128,128]{1,0:T(8,128)S(1)}, u32[]{:S(2)}, u32[]{:S(2)}) collective-permute-start(f32[128,128]{1,0:T(8,128)S(1)} %add.69), channel_id=1, source_target_pairs={{0,96},{16,112},{32,64},{48,80},{64,32},{80,48},{96,0},{112,16},{1... | collective-permute-start | bytes 196616 | tf_op jit(solution)/shard_map/ppermute | solution.py:185
  294.2 4.8 %collective-permute-start.4 = (f32[128,128]{1,0:T(8,128)S(1)}, f32[128,128]{1,0:T(8,128)S(1)}, u32[]{:S(2)}, u32[]{:S(2)}) collective-permute-start(f32[128,128]{1,0:T(8,128)S(1)} %add_add_fusion.2), channel_id=1, source_target_pairs={{0,1},{1,0},{2,3},{3,2},{4,5},{5,4},{6,7},{7,6},{8,9},{9,8},{10,11... | collective-permute-start | bytes 196616 | tf_op jit(solution)/shard_map/ppermute | solution.py:185
  295.7 5.9 %collective-permute-start.5 = (f32[128,128]{1,0:T(8,128)S(1)}, f32[128,128]{1,0:T(8,128)S(1)}, u32[]{:S(2)}, u32[]{:S(2)}) collective-permute-start(f32[128,128]{1,0:T(8,128)S(1)} %add_add_fusion.2), channel_id=1, source_target_pairs={{0,2},{1,3},{2,0},{3,1},{4,6},{5,7},{6,4},{7,5},{8,10},{9,11},{10,... | collective-permute-start | bytes 196616 | tf_op jit(solution)/shard_map/ppermute | solution.py:185
  298.5 5.5 %collective-permute-start.6 = (f32[128,128]{1,0:T(8,128)S(1)}, f32[128,128]{1,0:T(8,128)S(1)}, u32[]{:S(2)}, u32[]{:S(2)}) collective-permute-start(f32[128,128]{1,0:T(8,128)S(1)} %add_add_fusion.2), channel_id=1, source_target_pairs={{0,3},{1,2},{2,1},{3,0},{4,7},{5,6},{6,5},{7,4},{8,11},{9,10},{10,... | collective-permute-start | bytes 196616 | tf_op jit(solution)/shard_map/ppermute | solution.py:185
  304.0 4.8 %collective-permute-start.7 = (f32[128,128]{1,0:T(8,128)S(1)}, f32[128,128]{1,0:T(8,128)S(1)}, u32[]{:S(2)}, u32[]{:S(2)}) collective-permute-start(f32[128,128]{1,0:T(8,128)S(1)} %add_add_fusion.1), channel_id=1, source_target_pairs={{0,4},{1,5},{2,6},{3,7},{4,0},{5,1},{6,2},{7,3},{8,12},{9,13},{10,... | collective-permute-start | bytes 196616 | tf_op jit(solution)/shard_map/ppermute | solution.py:185
  305.6 5.8 %collective-permute-start.8 = (f32[128,128]{1,0:T(8,128)S(1)}, f32[128,128]{1,0:T(8,128)S(1)}, u32[]{:S(2)}, u32[]{:S(2)}) collective-permute-start(f32[128,128]{1,0:T(8,128)S(1)} %add_add_fusion.1), channel_id=1, source_target_pairs={{0,8},{1,9},{2,10},{3,11},{4,12},{5,13},{6,14},{7,15},{8,0},{9,1},... | collective-permute-start | bytes 196616 | tf_op jit(solution)/shard_map/ppermute | solution.py:185
  308.4 5.5 %collective-permute-start.9 = (f32[128,128]{1,0:T(8,128)S(1)}, f32[128,128]{1,0:T(8,128)S(1)}, u32[]{:S(2)}, u32[]{:S(2)}) collective-permute-start(f32[128,128]{1,0:T(8,128)S(1)} %add_add_fusion.1), channel_id=1, source_target_pairs={{0,12},{1,13},{2,14},{3,15},{4,8},{5,9},{6,10},{7,11},{8,4},{9,5},... | collective-permute-start | bytes 196616 | tf_op jit(solution)/shard_map/ppermute | solution.py:185

commit v2 on v1

v2 whole, which is shorter than its diff:
```python
import jax
import jax.numpy as jnp
from jax import lax
from jax.experimental import pallas as pl
from jax.experimental.pallas import tpu as pltpu
from jax.sharding import PartitionSpec as P

W = 128
damping = 0.5
AXES = ("elem", "vox")
BF, F32 = jnp.bfloat16, jnp.float32

FIRST = ((0, 0), (0, 1), (1, 0))
SECOND = ((1, 1),)
TILES_PER_STEP = 16


def window_kernel(seen_hbm, start_ref, taps_ref, echo_ref, first_ref, second_ref, base_ref, band_ref, seen_ref, sem):
    step = pl.program_id(0)
    members = base_ref.shape[0]
    planes = base_ref.shape[1]
    fetch = pltpu.make_async_copy(seen_hbm, seen_ref, sem)

    @pl.when(step == 0)
    def _():
        fetch.start()
        taps = taps_ref[...].astype(F32)
        offset = lax.broadcasted_iota(jnp.int32, (640, 128), 0) - 4 * lax.broadcasted_iota(jnp.int32, (640, 128), 1)
        for c in range(2):
            band = jnp.zeros((640, 128), F32)
            for k in range(taps.shape[1]):
                band = jnp.where(offset == k, taps[c : c + 1, k : k + 1], band)
            band_ref[:, 128 * c : 128 * c + 128] = band.astype(BF)

    @pl.when(step < members)
    def _():
        rows = []
        for plane in range(planes):
            x = echo_ref[0, plane]
            x = jnp.concatenate([x, jnp.zeros((x.shape[0], 128), x.dtype)], axis=1)
            for j in range(4):
                rows.append(x[:, 512 * j : 512 * j + 640])
        out = jnp.dot(jnp.concatenate(rows, axis=0), band_ref[...], preferred_element_type=F32)
        out = out.astype(BF).astype(F32)
        for plane in range(planes):
            for j in range(4):
                r = 64 * (4 * plane + j)
                base_ref[step, plane, j, 0:64, :] = out[r : r + 64, 0:128]
                base_ref[step, plane, j, 64:128, :] = out[r : r + 64, 128:256]

    @pl.when(step == members)
    def _():
        fetch.wait()

    @pl.when(step >= members)
    def _():
        lane = lax.broadcasted_iota(jnp.int32, (128, 128), 1)
        me = lax.axis_index(AXES)
        for i in range(TILES_PER_STEP):
            tile = (step - members) * TILES_PER_STEP + i
            for ref, units in ((first_ref, FIRST), (second_ref, SECOND)):
                for k, (slot, plane) in enumerate(units):
                    seen = seen_ref[tile * 2 + slot, me]
                    member = jnp.maximum(seen, 0)
                    start = start_ref[plane * 2 + slot, tile]
                    block = start // 128
                    shift = start - 128 * block
                    here = base_ref[member, plane, block]
                    after = base_ref[member, plane, jnp.minimum(block + 1, 3)]
                    both = jnp.where(lane >= shift, here, after)
                    out = pltpu.roll(both, (128 - shift) & 127, 1)
                    ref[i, k] = jnp.where(seen >= 0, out, 0.0).astype(BF)


def make_windows(echoes, taps, seen, starts):
    members, planes, frames, samples = echoes.shape
    tiles = starts.shape[1]
    steps = members + tiles // TILES_PER_STEP
    last = members - 1

    def out_map(i):
        return (jnp.maximum(i - members, 0), 0, 0, 0)

    return pl.pallas_call(
        window_kernel,
        grid=(steps,),
        in_specs=[
            pl.BlockSpec(memory_space=pl.ANY),
            pl.BlockSpec(memory_space=pltpu.SMEM),
            pl.BlockSpec(taps.shape, lambda i: (0, 0)),
            pl.BlockSpec((1, planes, frames, samples), lambda i: (jnp.minimum(i, last), 0, 0, 0)),
        ],
        out_specs=[pl.BlockSpec((TILES_PER_STEP, len(units), 128, 128), out_map) for units in (FIRST, SECOND)],
        scratch_shapes=[
            pltpu.VMEM((members, planes, 4, 128, 128), F32),
            pltpu.VMEM((640, 256), BF),
            pltpu.SMEM(seen.shape, jnp.int32),
            pltpu.SemaphoreType.DMA,
        ],
        out_shape=[jax.ShapeDtypeStruct((tiles, len(units), 128, 128), BF) for units in (FIRST, SECOND)],
        compiler_params=pltpu.CompilerParams(vmem_limit_bytes=60 * 2**20),
        cost_estimate=pl.CostEstimate(flops=2 * 10**9, bytes_accessed=20 * 2**20, transcendentals=0),
        name="windows",
    )(seen, starts, taps, echoes)


def weights(lag):
    lag = jnp.broadcast_to(lag.astype(F32) * 0.25 - 64.0, (16, lag.shape[1])).astype(BF)
    iota = lax.broadcasted_iota(jnp.int32, (16, 128), 0).astype(F32)
    one, zero = jnp.ones((), BF), jnp.zeros((), BF)
    columns = []
    for c in range(lag.shape[1] // 128):
        d = lag[:, 128 * c : 128 * c + 128]
        columns.append(
            jnp.concatenate(
                [jnp.maximum(one - jnp.abs(d - (iota + (16.0 * w - 64.0)).astype(BF)), zero) for w in range(8)], axis=0
            )
        )
    return jnp.concatenate(columns, axis=1)


def accumulate(units, group, windows_ref, lag_ref, acc_ref):
    todo = [(b, k) for b in range(group) for k in range(len(units))]
    for at in range(0, len(todo), 2):
        pair = todo[at : at + 2]
        lhs = jnp.concatenate([windows_ref[b, k] for b, k in pair], axis=1)
        for v in range(0, acc_ref.shape[1], 256):
            rhs = []
            for b, k in pair:
                slot, plane = units[k]
                rhs.append(weights(lag_ref[plane, b, slot : slot + 1, v : v + 256]))
            acc_ref[:, v : v + 256] += jnp.dot(lhs, jnp.concatenate(rhs, axis=0), preferred_element_type=F32)


def first_beam_kernel(units, group, lag_ref, windows_ref, out_ref):
    @pl.when(pl.program_id(0) == 0)
    def _():
        out_ref[...] = jnp.zeros_like(out_ref)

    accumulate(units, group, windows_ref, lag_ref, out_ref)


def second_beam_kernel(units, group, gain_ref, lag_ref, windows_ref, before_ref, out_ref, gram_ref):
    @pl.when(pl.program_id(0) == 0)
    def _():
        out_ref[...] = before_ref[...]

    accumulate(units, group, windows_ref, lag_ref, out_ref)

    @pl.when(pl.program_id(0) == pl.num_programs(0) - 1)
    def _():
        beam = out_ref[...] * gain_ref[0]
        out_ref[...] = beam
        gram_ref[...] = lax.dot_general(
            beam, beam, (((1,), (1,)), ((), ())), precision=lax.Precision.HIGHEST, preferred_element_type=F32
        )


def beam_call(units, group, lags, windows, gain=None, before=None):
    planes, blocks, slots, voxels = lags.shape
    body = second_beam_kernel if before is not None else first_beam_kernel
    in_specs = [
        pl.BlockSpec((planes, group, slots, voxels), lambda i: (0, i, 0, 0)),
        pl.BlockSpec((group, len(units), 128, 128), lambda i: (i, 0, 0, 0)),
    ]
    args = [lags, windows]
    whole = pl.BlockSpec((128, voxels), lambda i: (0, 0))
    out_shape = [jax.ShapeDtypeStruct((128, voxels), F32)]
    out_specs = [whole]
    if before is not None:
        in_specs = [pl.BlockSpec(memory_space=pltpu.SMEM)] + in_specs + [whole]
        args = [gain] + args + [before]
        out_shape.append(jax.ShapeDtypeStruct((128, 128), F32))
        out_specs.append(pl.BlockSpec((128, 128), lambda i: (0, 0)))

    def kernel(*refs):
        body(units, group, *refs)

    return pl.pallas_call(
        kernel,
        grid=(blocks // group,),
        in_specs=in_specs,
        out_specs=out_specs,
        out_shape=out_shape,
        compiler_params=pltpu.CompilerParams(vmem_limit_bytes=48 * 2**20),
        cost_estimate=pl.CostEstimate(
            flops=2 * 128 * voxels * 128 * blocks * len(units),
            bytes_accessed=blocks * len(units) * (128 * 256 + 8 * voxels),
            transcendentals=0,
        ),
        name="beam",
    )(*args)


def invert(a):
    n = a.shape[0]
    lane = lax.broadcasted_iota(jnp.int32, (n, n), 1)
    lane_row = lane[:1]
    sub = lax.broadcasted_iota(jnp.int32, (8, n), 0)
    for k in range(0, n, 2):
        row0, row1 = a[k : k + 1, :], a[k + 1 : k + 2, :]
        col0 = jnp.broadcast_to(a[:, k : k + 1], (n, n))
        col1 = jnp.broadcast_to(a[:, k + 1 : k + 2], (n, n))
        p00, p01 = col0[k : k + 1], col1[k : k + 1]
        p10, p11 = col0[k + 1 : k + 2], col1[k + 1 : k + 2]
        over = 1.0 / (p00 * p11 - p01 * p10)
        i00, i01, i10, i11 = p11 * over, -p01 * over, -p10 * over, p00 * over
        new0 = jnp.where(lane_row == k, i00, jnp.where(lane_row == k + 1, i01, i00 * row0 + i01 * row1))
        new1 = jnp.where(lane_row == k, i10, jnp.where(lane_row == k + 1, i11, i10 * row0 + i11 * row1))
        a = jnp.where((lane == k) | (lane == k + 1), 0.0, a) - col0 * new0 - col1 * new1
        g = k // 8 * 8
        fixed = jnp.where(sub == k - g, new0, jnp.where(sub == k + 1 - g, new1, a[g : g + 8]))
        a = jnp.concatenate([part for part in (a[:g], fixed, a[g + 8 :]) if part.shape[0]], axis=0)
    return a


def power_kernel(samples, gram_ref, beam_ref, out_ref):
    n = gram_ref.shape[0]
    gram = gram_ref[...]
    eye = lax.broadcasted_iota(jnp.int32, (n, n), 0) == lax.broadcasted_iota(jnp.int32, (n, n), 1)
    energy = jnp.sum(jnp.where(eye, gram, 0.0), keepdims=True)
    correlation = gram * (n / energy)
    filter_matrix = damping * invert(correlation + jnp.where(eye, damping, 0.0))
    filtered = lax.dot_general(
        filter_matrix,
        beam_ref[...],
        (((0,), (0,)), ((), ())),
        precision=lax.Precision.HIGHEST,
        preferred_element_type=F32,
    ) / jnp.sqrt(energy / samples)
    out_ref[...] = jnp.log(jnp.sum(filtered * filtered, axis=0, keepdims=True) / n + 1e-06)


def doppler_power(samples, gram, beam):
    def kernel(*refs):
        power_kernel(samples, *refs)

    return pl.pallas_call(
        kernel,
        out_shape=jax.ShapeDtypeStruct((1, beam.shape[1]), F32),
        compiler_params=pltpu.CompilerParams(vmem_limit_bytes=48 * 2**20),
        name="power",
    )(gram, beam)


def exchange_sum(x):
    for axis, digits in (("elem", (1,)), ("elem", (2, 4, 6)), ("vox", (1, 2, 3)), ("vox", (4, 8, 12))):
        size = lax.axis_size(axis)
        parts = [lax.ppermute(x, axis, [(i, i ^ k) for i in range(size)]) for k in digits]
        for part in parts:
            x = x + part
    return x


def shards(echoes, filter_taps, visible, window_start, delays, tile_gain):
    members, planes, frames, samples = echoes.shape
    channels = 2 * frames
    device_count = lax.axis_size("elem") * lax.axis_size("vox")
    voxels = delays.shape[-1]

    seen = jnp.transpose(visible, (0, 2, 1)).reshape(-1, visible.shape[1])
    starts = jnp.transpose(window_start[:, :, 0, :], (0, 2, 1)).reshape(-1, window_start.shape[1])
    first, second = make_windows(echoes, filter_taps, seen, starts)

    first = lax.all_to_all(first, AXES, split_axis=0, concat_axis=0, tiled=True)
    second = lax.all_to_all(second, AXES, split_axis=0, concat_axis=0, tiled=True)
    lags = delays[:, 0]
    (partial,) = beam_call(FIRST, 4, lags, first)
    beam, local_gram = beam_call(SECOND, 8, lags, second, tile_gain, partial)

    frame_gram = exchange_sum(local_gram)
    return doppler_power(channels * device_count * voxels, frame_gram, beam)


def solution(mesh):
    placed = (
        P(AXES, None, None, None),
        P(),
        P(),
        P(None, None, AXES, None),
        P(None, AXES, None, None, None),
        P(AXES),
    )
    return jax.shard_map(
        shards, mesh=mesh, in_specs=placed, out_specs=P(AXES, None), check_vma=False
    )
```

time: 342 us -> 280 us (0.82)
  Pallas kernels: 114 us -> 72.6 us
  other arithmetic: 24.4 us -> 0.06 us
  waiting for transfers between devices: 16.3 us -> 30.4 us
  local copies, waits for them, and re-layouts: 9.32 us -> 2.02 us
    pallas_call x2, Pallas kernels: 90.4 us -> 45.8 us  [beam_call(): pl.pallas_call(kernel, grid=(blocks // group,), in_specs=in_specs, out_sp...]
    another operation x5 -> x0, other arithmetic: 22.9 us -> none  [the longest x3 12.5 us: shards(): factor = jnp.linalg.cholesky(correlation + damping * identity)]
    all_to_all x1, waiting for transfers between devices: 0.01 us -> 17.8 us  [shards(): lax.all_to_all(second, AXES, split_axis=0, concat_axis=0, tiled=True)]
    ppermute x10, waiting for transfers between devices: 16.3 us -> 12.6 us  [exchange_sum(): lax.ppermute(x, axis, [(i, i ^ k) for i in range(size)])]
    pallas_call x1 -> x2, Pallas kernels: 23.9 us -> 26.7 us  [the longest x1 17.3 us: make_windows(): pl.pallas_call(window_kernel, grid=(steps,), in_specs=[pl.BlockSpec(memor...]
  transfers between devices with their start and end apart: 11 -> 11, of which waited for: 7 -> 8; matrix products, arithmetic and copies ran while one was open for 0% -> 0% of each run, Pallas kernels for 19% -> 11%
where the time goes in v2:
time: 280 us; the launch traced here: 279 us
  blocking collectives  152 us (54%)
  Pallas kernels  72.6 us (26%)
  waiting for transfers between devices  30.4 us (11%)
  starting transfers between devices  21.1 us (8%)
    all_to_all x1, blocking collectives, shards(): first = lax.all_to_all(first, AXES, split_axis=0, concat_axis=0, tiled=True)  152 us
    pallas_call x2, Pallas kernels, beam_call(): pl.pallas_call(kernel, grid=(blocks // group,), in_specs=in_specs, out_sp...  45.8 us
    all_to_all x1, waiting for transfers between devices, shards(): lax.all_to_all(second, AXES, split_axis=0, concat_axis=0, tiled=True)  17.8 us
    pallas_call x1, Pallas kernels, make_windows(): pl.pallas_call(window_kernel, grid=(steps,), in_specs=[pl.BlockSpec(memor...  17.3 us
    ppermute x10, starting transfers between devices, exchange_sum(): lax.ppermute(x, axis, [(i, i ^ k) for i in range(size)])  14.7 us
    ppermute x10, waiting for transfers between devices, exchange_sum(): lax.ppermute(x, axis, [(i, i ^ k) for i in range(size)])  12.6 us
    pallas_call x1, Pallas kernels, doppler_power(): pl.pallas_call(kernel, out_shape=jax.ShapeDtypeStruct((1, beam.shape[1]),...  9.44 us
    all_to_all x1, starting transfers between devices, shards(): lax.all_to_all(second, AXES, split_axis=0, concat_axis=0, tiled=True)  6.42 us
  transfers between devices with their start and end apart: 11, of which 8 were waited for; matrix products, arithmetic and copies ran while one was open for 0% of the time, Pallas kernels for 11%

profile of v2, /device:TPU:0, one launch (start us, length us, event | category | flops | bytes accessed | tf_op | source)
XLA Modules:
  0.0 279.1 jit_solution(15859556125429325591)
XLA Ops:
  0.0 17.3 %windows.1 = (bf16[128,3,128,128]{3,2,1,0:T(8,128)(2,1)}, bf16[128,1,128,128]{3,2,1,0:T(8,128)(2,1)}) custom-call(s32[256,128]{1,0:T(8,128)} %bitcast.11, s32[4,128]{1,0:T(4,128)} %bitcast.12, bf16[2,16]{1,0:T(2,128)(2,1)} %taps_ref.1, bf16[8,2,64,2048]{3,2,1,0:T(8,128)(2,1)} %echo_ref.1), custom_call_target="tpu_custom_call" | custom-call | flops 2000000000 | bytes 20971520 | tf_op jit(solution)/shard_map/windows/pallas_call | solution.py:84
  17.3 152.2 %all_to_all.10.refs_1_ = bf16[128,3,128,128]{3,2,1,0:T(8,128)(2,1)} all-to-all(bf16[128,3,128,128]{3,2,1,0:T(8,128)(2,1)} %get-tuple-element.10), channel_id=1, replica_groups=mesh['elem'=8,'vox'=16] {'elem','vox'}, dimensions={0} | all-to-all | bytes 25165824 | tf_op jit(solution)/shard_map/all_to_all | solution.py:265
  169.5 0.0 copy-start
  169.5 6.4 %all-to-all-start = ((bf16[128,1,128,128]{3,2,1,0:T(8,128)(2,1)}), bf16[128,1,128,128]{3,2,1,0:T(8,128)(2,1)}, u32[]{:S(2)}, u32[]{:S(2)}) async-start(bf16[128,1,128,128]{3,2,1,0:T(8,128)(2,1)} %get-tuple-element.9), calls=%async_computation | async-start | bytes 8388608 | tf_op jit(solution)/shard_map/all_to_all | solution.py:266
  176.6 0.0 copy-done
  176.6 31.3 %beam.2.refs_3_ = f32[128,1536]{1,0:T(8,128)S(1)} custom-call(s32[2,128,2,1536]{3,2,1,0:T(2,128)S(1)} %bitcast.9, bf16[128,3,128,128]{3,2,1,0:T(8,128)(2,1)} %all_to_all.10.refs_1_), custom_call_target="tpu_custom_call" | custom-call | flops 19327352832 | bytes 17301504 | tf_op jit(solution)/shard_map/beam/pallas_call | solution.py:179
  207.9 0.0 copy-start.1
  207.9 0.9 copy-done.1
  208.8 17.8 %all-to-all-done.refs_2_ = bf16[128,1,128,128]{3,2,1,0:T(8,128)(2,1)} async-done(((bf16[128,1,128,128]{3,2,1,0:T(8,128)(2,1)}), bf16[128,1,128,128]{3,2,1,0:T(8,128)(2,1)}, u32[]{:S(2)}, u32[]{:S(2)}) %all-to-all-start) | async-done | bytes 4194336 | tf_op jit(solution)/shard_map/all_to_all | solution.py:266
  226.6 0.0 copy-start.2
  226.6 1.1 copy-done.2
  227.7 14.6 %beam.3 = (f32[128,1536]{1,0:T(8,128)S(1)}, f32[128,128]{1,0:T(8,128)S(1)}) custom-call(f32[1]{0:T(128)S(6)} %copy.7.refs_0_, s32[2,128,2,1536]{3,2,1,0:T(2,128)S(1)} %bitcast.10, bf16[128,1,128,128]{3,2,1,0:T(8,128)(2,1)} %all-to-all-done.refs_2_, f32[128,1536]{1,0:T(8,128)S(1)} %copy-done.2), custom_call_target="tpu_custom_call" | custom-call | flops 6442450944 | bytes 5767168 | tf_op jit(solution)/shard_map/beam/pallas_call | solution.py:179
  242.3 0.4 collective-permute-start
  242.6 1.0 collective-permute-done
  243.6 1.0 collective-permute-start.1
  244.6 2.8 %collective-permute-start.2 = (f32[128,128]{1,0:T(8,128)S(1)}, f32[128,128]{1,0:T(8,128)S(1)}, u32[]{:S(2)}, u32[]{:S(2)}) collective-permute-start(f32[128,128]{1,0:T(8,128)S(1)} %add.30), channel_id=1, source_target_pairs={{0,64},{16,80},{32,96},{48,112},{64,0},{80,16},{96,32},{112,48},{1... | collective-permute-start | bytes 196616 | tf_op jit(solution)/shard_map/ppermute | solution.py:249
  247.4 1.0 collective-permute-start.3
  248.4 0.0 collective-permute-done.1
  248.4 2.5 collective-permute-done.2
  251.0 1.9 collective-permute-done.3
  252.9 0.8 collective-permute-start.4
  253.7 2.3 collective-permute-start.5
  256.0 1.7 collective-permute-start.6
  257.7 0.0 collective-permute-done.4
  257.7 1.9 collective-permute-done.5
  259.6 1.9 collective-permute-done.6
  261.5 0.7 collective-permute-start.7
  262.1 2.0 collective-permute-start.8
  264.2 2.0 collective-permute-start.9
  266.2 0.0 collective-permute-done.7
  266.2 1.7 collective-permute-done.8
  267.9 1.8 collective-permute-done.9
  269.7 9.4 %power.1 = f32[1,1536]{1,0:T(1,128)} custom-call(f32[128,128]{1,0:T(8,128)S(1)} %add_add_fusion.refs_0_, f32[128,1536]{1,0:T(8,128)S(1)} %get-tuple-element.12.refs_1_), custom_call_target="tpu_custom_call" | custom-call | tf_op jit(solution)/shard_map/power/pallas_call | solution.py:238
  (4 shorter events, 0.1 us)
Async XLA Ops:
  169.5 7.1 %copy-start = (s32[2,1,128,2,1536]{4,3,2,1,0:T(2,128)S(1)}, s32[2,1,128,2,1536]{4,3,2,1,0:T(2,128)}, u32[]{:S(2)}) copy-start(s32[2,1,128,2,1536]{4,3,2,1,0:T(2,128)} %param.10) | copy-start | bytes 9437188
  169.5 57.1 %all-to-all-start = ((bf16[128,1,128,128]{3,2,1,0:T(8,128)(2,1)}), bf16[128,1,128,128]{3,2,1,0:T(8,128)(2,1)}, u32[]{:S(2)}, u32[]{:S(2)}) async-start(bf16[128,1,128,128]{3,2,1,0:T(8,128)(2,1)} %get-tuple-element.9), calls=%async_computation | async-start | bytes 8388608 | tf_op jit(solution)/shard_map/all_to_all | solution.py:266
  207.9 0.9 copy-start.1
  226.6 1.1 copy-start.2
  242.3 1.3 collective-permute-start
  243.6 4.8 %collective-permute-start.1 = (f32[128,128]{1,0:T(8,128)S(1)}, f32[128,128]{1,0:T(8,128)S(1)}, u32[]{:S(2)}, u32[]{:S(2)}) collective-permute-start(f32[128,128]{1,0:T(8,128)S(1)} %add.30), channel_id=1, source_target_pairs={{0,32},{16,48},{32,0},{48,16},{64,96},{80,112},{96,64},{112,80},{1... | collective-permute-start | bytes 196616 | tf_op jit(solution)/shard_map/ppermute | solution.py:249
  244.6 6.4 %collective-permute-start.2 = (f32[128,128]{1,0:T(8,128)S(1)}, f32[128,128]{1,0:T(8,128)S(1)}, u32[]{:S(2)}, u32[]{:S(2)}) collective-permute-start(f32[128,128]{1,0:T(8,128)S(1)} %add.30), channel_id=1, source_target_pairs={{0,64},{16,80},{32,96},{48,112},{64,0},{80,16},{96,32},{112,48},{1... | collective-permute-start | bytes 196616 | tf_op jit(solution)/shard_map/ppermute | solution.py:249
  247.4 5.5 %collective-permute-start.3 = (f32[128,128]{1,0:T(8,128)S(1)}, f32[128,128]{1,0:T(8,128)S(1)}, u32[]{:S(2)}, u32[]{:S(2)}) collective-permute-start(f32[128,128]{1,0:T(8,128)S(1)} %add.30), channel_id=1, source_target_pairs={{0,96},{16,112},{32,64},{48,80},{64,32},{80,48},{96,0},{112,16},{1... | collective-permute-start | bytes 196616 | tf_op jit(solution)/shard_map/ppermute | solution.py:249
  252.9 4.8 %collective-permute-start.4 = (f32[128,128]{1,0:T(8,128)S(1)}, f32[128,128]{1,0:T(8,128)S(1)}, u32[]{:S(2)}, u32[]{:S(2)}) collective-permute-start(f32[128,128]{1,0:T(8,128)S(1)} %add_add_fusion.2), channel_id=1, source_target_pairs={{0,1},{1,0},{2,3},{3,2},{4,5},{5,4},{6,7},{7,6},{8,9},{9,8},{10,11... | collective-permute-start | bytes 196616 | tf_op jit(solution)/shard_map/ppermute | solution.py:249
  253.7 5.9 %collective-permute-start.5 = (f32[128,128]{1,0:T(8,128)S(1)}, f32[128,128]{1,0:T(8,128)S(1)}, u32[]{:S(2)}, u32[]{:S(2)}) collective-permute-start(f32[128,128]{1,0:T(8,128)S(1)} %add_add_fusion.2), channel_id=1, source_target_pairs={{0,2},{1,3},{2,0},{3,1},{4,6},{5,7},{6,4},{7,5},{8,10},{9,11},{10,... | collective-permute-start | bytes 196616 | tf_op jit(solution)/shard_map/ppermute | solution.py:249
  256.0 5.5 %collective-permute-start.6 = (f32[128,128]{1,0:T(8,128)S(1)}, f32[128,128]{1,0:T(8,128)S(1)}, u32[]{:S(2)}, u32[]{:S(2)}) collective-permute-start(f32[128,128]{1,0:T(8,128)S(1)} %add_add_fusion.2), channel_id=1, source_target_pairs={{0,3},{1,2},{2,1},{3,0},{4,7},{5,6},{6,5},{7,4},{8,11},{9,10},{10,... | collective-permute-start | bytes 196616 | tf_op jit(solution)/shard_map/ppermute | solution.py:249
  261.5 4.8 %collective-permute-start.7 = (f32[128,128]{1,0:T(8,128)S(1)}, f32[128,128]{1,0:T(8,128)S(1)}, u32[]{:S(2)}, u32[]{:S(2)}) collective-permute-start(f32[128,128]{1,0:T(8,128)S(1)} %add_add_fusion.1), channel_id=1, source_target_pairs={{0,4},{1,5},{2,6},{3,7},{4,0},{5,1},{6,2},{7,3},{8,12},{9,13},{10,... | collective-permute-start | bytes 196616 | tf_op jit(solution)/shard_map/ppermute | solution.py:249
  262.1 5.8 %collective-permute-start.8 = (f32[128,128]{1,0:T(8,128)S(1)}, f32[128,128]{1,0:T(8,128)S(1)}, u32[]{:S(2)}, u32[]{:S(2)}) collective-permute-start(f32[128,128]{1,0:T(8,128)S(1)} %add_add_fusion.1), channel_id=1, source_target_pairs={{0,8},{1,9},{2,10},{3,11},{4,12},{5,13},{6,14},{7,15},{8,0},{9,1},... | collective-permute-start | bytes 196616 | tf_op jit(solution)/shard_map/ppermute | solution.py:249
  264.2 5.5 %collective-permute-start.9 = (f32[128,128]{1,0:T(8,128)S(1)}, f32[128,128]{1,0:T(8,128)S(1)}, u32[]{:S(2)}, u32[]{:S(2)}) collective-permute-start(f32[128,128]{1,0:T(8,128)S(1)} %add_add_fusion.1), channel_id=1, source_target_pairs={{0,12},{1,13},{2,14},{3,15},{4,8},{5,9},{6,10},{7,11},{8,4},{9,5},... | collective-permute-start | bytes 196616 | tf_op jit(solution)/shard_map/ppermute | solution.py:249

commit v3 on v2

v3 whole, which is shorter than its diff:
```python
import jax
import jax.numpy as jnp
from jax import lax
from jax.experimental import pallas as pl
from jax.experimental.pallas import tpu as pltpu
from jax.sharding import PartitionSpec as P

W = 128
damping = 0.5
AXES = ("elem", "vox")
BF, F32 = jnp.bfloat16, jnp.float32

FIRST = ((0, 0), (0, 1), (1, 0))
SECOND = ((1, 1),)
TILES_PER_STEP = 32
MEMBERS_PER_STEP = 2
LIST_GROUP = 8


def window_kernel(seen_hbm, start_ref, taps_ref, echo_ref, first_ref, second_ref, base_ref, band_ref, seen_ref, sem):
    step = pl.program_id(0)
    demod_steps = base_ref.shape[0] // MEMBERS_PER_STEP
    planes = base_ref.shape[1]
    fetch = pltpu.make_async_copy(seen_hbm, seen_ref, sem)

    @pl.when(step == 0)
    def _():
        fetch.start()
        taps = taps_ref[...].astype(F32)
        offset = lax.broadcasted_iota(jnp.int32, (640, 128), 0) - 4 * lax.broadcasted_iota(jnp.int32, (640, 128), 1)
        for c in range(2):
            band = jnp.zeros((640, 128), F32)
            for k in range(taps.shape[1]):
                band = jnp.where(offset == k, taps[c : c + 1, k : k + 1], band)
            band_ref[:, 128 * c : 128 * c + 128] = band.astype(BF)

    @pl.when(step < demod_steps)
    def _():
        for m in range(MEMBERS_PER_STEP):
            rows = []
            for plane in range(planes):
                x = echo_ref[m, plane]
                x = jnp.concatenate([x, jnp.zeros((x.shape[0], 128), x.dtype)], axis=1)
                for j in range(4):
                    rows.append(x[:, 512 * j : 512 * j + 640])
            out = jnp.dot(jnp.concatenate(rows, axis=0), band_ref[...], preferred_element_type=F32)
            out = out.astype(BF).astype(F32)
            for plane in range(planes):
                for j in range(4):
                    r = 64 * (4 * plane + j)
                    base_ref[MEMBERS_PER_STEP * step + m, plane, j, 0:64, :] = out[r : r + 64, 0:128]
                    base_ref[MEMBERS_PER_STEP * step + m, plane, j, 64:128, :] = out[r : r + 64, 128:256]

    @pl.when(step == demod_steps)
    def _():
        fetch.wait()

    @pl.when(step >= demod_steps)
    def _():
        lane = lax.broadcasted_iota(jnp.int32, (128, 128), 1)
        me = lax.axis_index(AXES)
        for i in range(TILES_PER_STEP):
            tile = (step - demod_steps) * TILES_PER_STEP + i
            seen0 = seen_ref[tile * 2, me]
            seen1 = seen_ref[tile * 2 + 1, me]
            keep = seen0 >= 0
            seen_at = (jnp.where(keep, seen0, seen1), jnp.where(keep, seen1, -1))
            for ref, units in ((first_ref, FIRST), (second_ref, SECOND)):
                for k, (place, plane) in enumerate(units):
                    seen = seen_at[place]
                    start = start_ref[plane * 2 + 1, tile]
                    if place == 0:
                        start = jnp.where(keep, start_ref[plane * 2, tile], start)
                    member = jnp.maximum(seen, 0)
                    block = start // 128
                    shift = start - 128 * block
                    here = base_ref[member, plane, block]
                    after = base_ref[member, plane, jnp.minimum(block + 1, 3)]
                    both = jnp.where(lane >= shift, here, after)
                    out = pltpu.roll(both, (128 - shift) & 127, 1)
                    ref[i, k] = jnp.where(seen >= 0, out, 0.0).astype(BF)


def make_windows(echoes, taps, seen, starts):
    members, planes, frames, samples = echoes.shape
    tiles = starts.shape[1]
    demod_steps = members // MEMBERS_PER_STEP

    def out_map(i):
        return (jnp.maximum(i - demod_steps, 0), 0, 0, 0)

    return pl.pallas_call(
        window_kernel,
        grid=(demod_steps + tiles // TILES_PER_STEP,),
        in_specs=[
            pl.BlockSpec(memory_space=pl.ANY),
            pl.BlockSpec(memory_space=pltpu.SMEM),
            pl.BlockSpec(taps.shape, lambda i: (0, 0)),
            pl.BlockSpec(
                (MEMBERS_PER_STEP, planes, frames, samples), lambda i: (jnp.minimum(i, demod_steps - 1), 0, 0, 0)
            ),
        ],
        out_specs=[pl.BlockSpec((TILES_PER_STEP, len(units), 128, 128), out_map) for units in (FIRST, SECOND)],
        scratch_shapes=[
            pltpu.VMEM((members, planes, 4, 128, 128), F32),
            pltpu.VMEM((640, 256), BF),
            pltpu.SMEM(seen.shape, jnp.int32),
            pltpu.SemaphoreType.DMA,
        ],
        out_shape=[jax.ShapeDtypeStruct((tiles, len(units), 128, 128), BF) for units in (FIRST, SECOND)],
        compiler_params=pltpu.CompilerParams(vmem_limit_bytes=60 * 2**20),
        cost_estimate=pl.CostEstimate(flops=2 * 10**9, bytes_accessed=20 * 2**20, transcendentals=0),
        name="windows",
    )(seen, starts, taps, echoes)


def weights(lag):
    lag = jnp.broadcast_to(lag.astype(F32) * 0.25 - 64.0, (16, lag.shape[1])).astype(BF)
    iota = lax.broadcasted_iota(jnp.int32, (16, 128), 0).astype(F32)
    one, zero = jnp.ones((), BF), jnp.zeros((), BF)
    columns = []
    for c in range(lag.shape[1] // 128):
        d = lag[:, 128 * c : 128 * c + 128]
        columns.append(
            jnp.concatenate(
                [jnp.maximum(one - jnp.abs(d - (iota + (16.0 * w - 64.0)).astype(BF)), zero) for w in range(8)], axis=0
            )
        )
    return jnp.concatenate(columns, axis=1)


def add_pieces(pieces, acc_ref):
    for at in range(0, len(pieces), 2):
        pair = pieces[at : at + 2]
        lhs = jnp.concatenate([windows() for windows, lags in pair], axis=1)
        for v in range(0, acc_ref.shape[1], 256):
            rhs = jnp.concatenate([weights(lags(slice(v, v + 256))) for windows, lags in pair], axis=0)
            acc_ref[:, v : v + 256] += jnp.dot(lhs, rhs, preferred_element_type=F32)


def first_beam_kernel(group, swap_ref, lag_ref, windows_ref, out_ref):
    step = pl.program_id(0)

    @pl.when(step == 0)
    def _():
        out_ref[...] = jnp.zeros_like(out_ref)

    def piece(b, k, place, plane):
        def lags(voxels):
            kept = lag_ref[plane, b, place : place + 1, voxels]
            if place == 1:
                return kept
            return jnp.where(swap_ref[step * group + b] == 1, lag_ref[plane, b, 1:2, voxels], kept)

        return (lambda: windows_ref[b, k]), lags

    add_pieces([piece(b, k, *unit) for b in range(group) for k, unit in enumerate(FIRST)], out_ref)


def first_beam(group, swap, lags, windows):
    planes, blocks, slots, voxels = lags.shape
    units = len(FIRST)

    def kernel(*refs):
        first_beam_kernel(group, *refs)

    return pl.pallas_call(
        kernel,
        grid_spec=pltpu.PrefetchScalarGridSpec(
            num_scalar_prefetch=1,
            grid=(blocks // group,),
            in_specs=[
                pl.BlockSpec((planes, group, slots, voxels), lambda i, *_: (0, i, 0, 0)),
                pl.BlockSpec((group, units, 128, 128), lambda i, *_: (i, 0, 0, 0)),
            ],
            out_specs=pl.BlockSpec((128, voxels), lambda i, *_: (0, 0)),
        ),
        out_shape=jax.ShapeDtypeStruct((128, voxels), F32),
        compiler_params=pltpu.CompilerParams(vmem_limit_bytes=48 * 2**20),
        cost_estimate=pl.CostEstimate(
            flops=2 * 128 * voxels * 128 * blocks * units,
            bytes_accessed=blocks * units * (128 * 256 + 8 * voxels),
            transcendentals=0,
        ),
        name="beam",
    )(swap, lags, windows)


def second_beam_kernel(list_ref, gain_ref, lag_ref, *refs):
    window_refs = refs[:LIST_GROUP]
    before_hbm, out_ref, gram_ref, before_ref, sem = refs[LIST_GROUP:]
    step = pl.program_id(0)
    ((place, plane),) = SECOND
    fetch = pltpu.make_async_copy(before_hbm, before_ref, sem)

    @pl.when(step == 0)
    def _():
        fetch.start()
        out_ref[...] = jnp.zeros_like(out_ref)

    @pl.when(step * LIST_GROUP < list_ref[lag_ref.shape[1]])
    def _():
        def piece(j):
            block = list_ref[step * LIST_GROUP + j]
            return (lambda: window_refs[j][0, 0]), (lambda voxels: lag_ref[0, block, place : place + 1, voxels])

        add_pieces([piece(j) for j in range(LIST_GROUP)], out_ref)

    @pl.when(step == pl.num_programs(0) - 1)
    def _():
        fetch.wait()
        beam = (before_ref[...] + out_ref[...]) * gain_ref[0]
        out_ref[...] = beam
        high = beam.astype(BF)
        rest = beam - high.astype(F32)
        middle = rest.astype(BF)
        low = (rest - middle.astype(F32)).astype(BF)
        dims = (((1,), (1,)), ((), ()))
        stacked = jnp.concatenate([high, middle], axis=0)
        main = lax.dot_general(stacked, stacked, dims, preferred_element_type=F32)
        cross = main[:128, 128:] + lax.dot_general(high, low, dims, preferred_element_type=F32)
        gram_ref[...] = main[:128, :128] + (cross + cross.T + main[128:, 128:])


def second_beam(order, gain, lags, windows, before):
    planes, blocks, slots, voxels = lags.shape
    ((place, plane),) = SECOND
    steps = blocks // LIST_GROUP

    def window_spec(j):
        def index(i, order):
            last = jnp.maximum((order[blocks] + LIST_GROUP - 1) // LIST_GROUP - 1, 0)
            return (order[jnp.minimum(i, last) * LIST_GROUP + j], 0, 0, 0)

        return pl.BlockSpec((1, 1, 128, 128), index)

    return pl.pallas_call(
        second_beam_kernel,
        grid_spec=pltpu.PrefetchScalarGridSpec(
            num_scalar_prefetch=1,
            grid=(steps,),
            in_specs=[
                pl.BlockSpec(memory_space=pltpu.SMEM),
                pl.BlockSpec((1, blocks, slots, voxels), lambda i, *_: (plane, 0, 0, 0)),
            ]
            + [window_spec(j) for j in range(LIST_GROUP)]
            + [pl.BlockSpec(memory_space=pl.ANY)],
            out_specs=[
                pl.BlockSpec((128, voxels), lambda i, *_: (0, 0)),
                pl.BlockSpec((128, 128), lambda i, *_: (0, 0)),
            ],
            scratch_shapes=[pltpu.VMEM((128, voxels), F32), pltpu.SemaphoreType.DMA],
        ),
        out_shape=[jax.ShapeDtypeStruct((128, voxels), F32), jax.ShapeDtypeStruct((128, 128), F32)],
        compiler_params=pltpu.CompilerParams(vmem_limit_bytes=48 * 2**20),
        cost_estimate=pl.CostEstimate(
            flops=2 * 128 * voxels * 128 * blocks,
            bytes_accessed=blocks * (128 * 256 + 8 * voxels),
            transcendentals=0,
        ),
        name="beam",
    )(order, gain, lags, *([windows] * LIST_GROUP), before)


def live_order(seen):
    blocks = seen.shape[0]
    swap = ((seen[:, 0] < 0) & (seen[:, 1] >= 0)).astype(jnp.int32)
    key = 1 - ((seen[:, 0] >= 0) & (seen[:, 1] >= 0)).astype(jnp.int32)
    ids = jnp.arange(blocks, dtype=jnp.int32)
    key = key * blocks + ids
    rank = jnp.sum((key[None, :] < key[:, None]).astype(jnp.int32), axis=1)
    order = jnp.sum(jnp.where(rank[None, :] == ids[:, None], ids[None, :], 0), axis=1)
    count = jnp.sum((key < blocks).astype(jnp.int32), keepdims=True)
    return swap, jnp.concatenate([order, count])


def product2(x, y):
    return [[x[i][0] * y[0][j] + x[i][1] * y[1][j] for j in range(2)] for i in range(2)]


def inverse2(x):
    over = 1.0 / (x[0][0] * x[1][1] - x[0][1] * x[1][0])
    return [[x[1][1] * over, -x[0][1] * over], [-x[1][0] * over, x[0][0] * over]]


def inverse4(p):
    e, f, g, h = ([[p[r + i][c + j] for j in range(2)] for i in range(2)] for r in (0, 2) for c in (0, 2))
    e = inverse2(e)
    ge, ef = product2(g, e), product2(e, f)
    t = product2(g, ef)
    s = inverse2([[h[i][j] - t[i][j] for j in range(2)] for i in range(2)])
    right, left = product2(ef, s), product2(s, ge)
    t = product2(right, ge)
    top = [[e[i][0] + t[i][0], e[i][1] + t[i][1], -right[i][0], -right[i][1]] for i in range(2)]
    return top + [[-left[i][0], -left[i][1], s[i][0], s[i][1]] for i in range(2)]


def invert(a):
    n = a.shape[0]
    lane = lax.broadcasted_iota(jnp.int32, (n, n), 1)
    lane_row = lane[:1]
    sub = lax.broadcasted_iota(jnp.int32, (8, n), 0)
    for k in range(0, n, 4):
        rows = [a[k + i : k + i + 1, :] for i in range(4)]
        cols = [jnp.broadcast_to(a[:, k + i : k + i + 1], (n, n)) for i in range(4)]
        pivot = inverse4([[cols[j][k + i : k + i + 1] for j in range(4)] for i in range(4)])
        new = []
        for i in range(4):
            q = pivot[i]
            row = (q[0] * rows[0] + q[1] * rows[1]) + (q[2] * rows[2] + q[3] * rows[3])
            for j in range(4):
                row = jnp.where(lane_row == k + j, q[j], row)
            new.append(row)
        update = (cols[0] * new[0] + cols[1] * new[1]) + (cols[2] * new[2] + cols[3] * new[3])
        a = jnp.where((lane >= k) & (lane < k + 4), 0.0, a) - update
        g = k // 8 * 8
        fixed = a[g : g + 8]
        for i in range(4):
            fixed = jnp.where(sub == k + i - g, new[i], fixed)
        a = jnp.concatenate([part for part in (a[:g], fixed, a[g + 8 :]) if part.shape[0]], axis=0)
    return a


def power_kernel(samples, gram_ref, beam_ref, out_ref):
    n = gram_ref.shape[0]
    gram = gram_ref[...]
    eye = lax.broadcasted_iota(jnp.int32, (n, n), 0) == lax.broadcasted_iota(jnp.int32, (n, n), 1)
    energy = jnp.sum(jnp.where(eye, gram, 0.0), keepdims=True)
    correlation = gram * (n / energy)
    filter_matrix = damping * invert(correlation + jnp.where(eye, damping, 0.0))
    filtered = lax.dot_general(
        filter_matrix,
        beam_ref[...],
        (((0,), (0,)), ((), ())),
        precision=lax.Precision.HIGHEST,
        preferred_element_type=F32,
    ) / jnp.sqrt(energy / samples)
    out_ref[...] = jnp.log(jnp.sum(filtered * filtered, axis=0, keepdims=True) / n + 1e-06)


def doppler_power(samples, gram, beam):
    def kernel(*refs):
        power_kernel(samples, *refs)

    return pl.pallas_call(
        kernel,
        out_shape=jax.ShapeDtypeStruct((1, beam.shape[1]), F32),
        compiler_params=pltpu.CompilerParams(vmem_limit_bytes=48 * 2**20),
        name="power",
    )(gram, beam)


def exchange_sum(x):
    for axis, digits in (("elem", (1,)), ("elem", (2, 4, 6)), ("vox", (1, 2, 3)), ("vox", (4, 8, 12))):
        size = lax.axis_size(axis)
        parts = [lax.ppermute(x, axis, [(i, i ^ k) for i in range(size)]) for k in digits]
        for part in parts:
            x = x + part
    return x


def shards(echoes, filter_taps, visible, window_start, delays, tile_gain):
    members, planes, frames, samples = echoes.shape
    channels = 2 * frames
    device_count = lax.axis_size("elem") * lax.axis_size("vox")
    voxels = delays.shape[-1]

    seen = jnp.transpose(visible, (0, 2, 1)).reshape(-1, visible.shape[1])
    starts = jnp.transpose(window_start[:, :, 0, :], (0, 2, 1)).reshape(-1, window_start.shape[1])
    first, second = make_windows(echoes, filter_taps, seen, starts)

    first = lax.all_to_all(first, AXES, split_axis=0, concat_axis=0, tiled=True)
    second = lax.all_to_all(second, AXES, split_axis=0, concat_axis=0, tiled=True)
    visible, first = lax.optimization_barrier((visible, first))
    my_seen = lax.dynamic_index_in_dim(visible, lax.axis_index(AXES), 0, keepdims=False)
    swap, order = live_order(my_seen)
    lags = delays[:, 0]
    partial = first_beam(4, swap, lags, first)
    beam, local_gram = second_beam(order, tile_gain, lags, second, partial)

    frame_gram = exchange_sum(local_gram)
    return doppler_power(channels * device_count * voxels, frame_gram, beam)


def solution(mesh):
    placed = (
        P(AXES, None, None, None),
        P(),
        P(),
        P(None, None, AXES, None),
        P(None, AXES, None, None, None),
        P(AXES),
    )
    return jax.shard_map(
        shards, mesh=mesh, in_specs=placed, out_specs=P(AXES, None), check_vma=False
    )
```

time: 280 us -> 270 us (0.964)
  Pallas kernels: 72.6 us -> 64 us
  waiting for transfers between devices: 30.4 us -> 27.3 us
    pallas_call x3, Pallas kernels: 63.1 us -> 56 us  [the longest x1 32.4 us: first_beam(): pl.pallas_call(kernel, grid_spec=pltpu.PrefetchScalarGridSpec(num_scalar_...]
    all_to_all x1, waiting for transfers between devices: 17.8 us -> 14.4 us  [shards(): lax.all_to_all(second, AXES, split_axis=0, concat_axis=0, tiled=True)]
  transfers between devices with their start and end apart: 11 -> 11, of which waited for: 8 -> 9; matrix products, arithmetic and copies ran while one was open for 0% -> 1% of each run, Pallas kernels for 11% -> 12%
where the time goes in v3:
time: 270 us; the launch traced here: 268 us
  blocking collectives  152 us (56%)
  Pallas kernels  64 us (24%)
  waiting for transfers between devices  27.3 us (10%)
  starting transfers between devices  19 us (7%)
    all_to_all x1, blocking collectives, shards(): first = lax.all_to_all(first, AXES, split_axis=0, concat_axis=0, tiled=True)  152 us
    pallas_call x1, Pallas kernels, first_beam(): pl.pallas_call(kernel, grid_spec=pltpu.PrefetchScalarGridSpec(num_scalar_...  32.4 us
    all_to_all x1, waiting for transfers between devices, shards(): lax.all_to_all(second, AXES, split_axis=0, concat_axis=0, tiled=True)  14.4 us
    pallas_call x1, Pallas kernels, make_windows(): pl.pallas_call(window_kernel, grid=(demod_steps + tiles // TILES_PER_STEP...  14.3 us
    ppermute x10, waiting for transfers between devices, exchange_sum(): lax.ppermute(x, axis, [(i, i ^ k) for i in range(size)])  12.9 us
    ppermute x10, starting transfers between devices, exchange_sum(): lax.ppermute(x, axis, [(i, i ^ k) for i in range(size)])  12.6 us
    pallas_call x1, Pallas kernels, second_beam(): pl.pallas_call(second_beam_kernel, grid_spec=pltpu.PrefetchScalarGridSpec...  9.39 us
    pallas_call x1, Pallas kernels, doppler_power(): pl.pallas_call(kernel, out_shape=jax.ShapeDtypeStruct((1, beam.shape[1]),...  7.97 us
  transfers between devices with their start and end apart: 11, of which 9 were waited for; matrix products, arithmetic and copies ran while one was open for 1% of the time, Pallas kernels for 12%

profile of v3, /device:TPU:0, one launch (start us, length us, event | category | flops | bytes accessed | tf_op | source)
XLA Modules:
  0.0 267.7 jit_solution(1536719376249316349)
XLA Ops:
  0.0 14.3 %windows.1 = (bf16[128,3,128,128]{3,2,1,0:T(8,128)(2,1)}, bf16[128,1,128,128]{3,2,1,0:T(8,128)(2,1)}) custom-call(s32[256,128]{1,0:T(8,128)} %bitcast.22, s32[4,128]{1,0:T(4,128)} %bitcast.23, bf16[2,16]{1,0:T(2,128)(2,1)} %taps_ref.1, bf16[8,2,64,2048]{3,2,1,0:T(8,128)(2,1)} %echo_ref.1), custom_call_target="tpu_custom_call" | custom-call | flops 2000000000 | bytes 20971520 | tf_op jit(solution)/shard_map/windows/pallas_call | solution.py:92
  14.3 152.2 %all_to_all.10.refs_2_ = bf16[128,3,128,128]{3,2,1,0:T(8,128)(2,1)} all-to-all(bf16[128,3,128,128]{3,2,1,0:T(8,128)(2,1)} %get-tuple-element.11), channel_id=1, replica_groups=mesh['elem'=8,'vox'=16] {'elem','vox'}, dimensions={0} | all-to-all | bytes 25165824 | tf_op jit(solution)/shard_map/all_to_all | solution.py:372
  166.5 0.0 copy-start
  166.5 6.4 %all-to-all-start.1 = ((bf16[128,1,128,128]{3,2,1,0:T(8,128)(2,1)}), bf16[128,1,128,128]{3,2,1,0:T(8,128)(2,1)}, u32[]{:S(2)}, u32[]{:S(2)}) async-start(bf16[128,1,128,128]{3,2,1,0:T(8,128)(2,1)} %get-tuple-element.13), calls=%async_computation.1 | async-start | bytes 8388608 | tf_op jit(solution)/shard_map/all_to_all | solution.py:373
  173.6 0.7 dynamic-slice_bitcast_fusion
  174.3 0.6 bitcast_add_fusion
  174.9 0.2 convert_reduce_fusion
  175.1 0.1 select_reduce_fusion
  175.2 0.7 pad_add_fusion.list_ref
  175.9 0.0 copy-done
  175.9 32.4 %beam.2.refs_8_ = f32[128,1536]{1,0:T(8,128)S(1)} custom-call(s32[128]{0:T(128)S(1)} %fusion.1.refs_0_, s32[2,128,2,1536]{3,2,1,0:T(2,128)S(1)} %bitcast.20, bf16[128,3,128,128]{3,2,1,0:T(8,128)(2,1)} %all_to_all.10.refs_2_), custom_call_target="tpu_custom_call" | custom-call | flops 19327352832 | bytes 17301504 | tf_op jit(solution)/shard_map/beam/pallas_call | solution.py:167
  208.3 0.0 copy-start.1
  208.3 0.9 copy-done.1
  209.2 14.4 %all-to-all-done.1.refs_0_.refs_1_.refs_2_.refs_3_.refs_4_.refs_5_.refs_6_.refs_7_ = bf16[128,1,128,128]{3,2,1,0:T(8,128)(2,1)} async-done(((bf16[128,1,128,128]{3,2,1,0:T(8,128)(2,1)}), bf16[128,1,128,128]{3,2,1,0:T(8,128)(2,1)}, u32[]{:S(2)}, u32[]{:S(2)}) %all-to-all-start.1) | async-done | bytes 4194336 | tf_op jit(solution)/shard_map/all_to_all | solution.py:373
  223.6 0.0 copy-start.2
  223.6 1.1 copy-done.2
  224.7 9.4 %beam.3 = (f32[128,1536]{1,0:T(8,128)S(1)}, f32[128,128]{1,0:T(8,128)S(1)}) custom-call(s32[129]{0:T(256)S(1)} %pad_add_fusion.list_ref, f32[1]{0:T(128)S(6)} %copy.7.gain_ref, s32[2,128,2,1536]{3,2,1,0:T(2,128)S(1)} %bitcast.21, bf16[128,1,128,128]{3,2,1,0:T(8,128)(2,1)} %all-to-all-done.1.refs_0_.refs_1_.refs_2_.refs_3_.refs_4_.refs_5_.refs_6_.refs_7_, ...), custom_call_target="tpu_custom_call" | custom-call | flops 6442450944 | bytes 5767168 | tf_op jit(solution)/shard_map/beam/pallas_call | solution.py:237
  234.1 0.1 collective-permute-start
  234.2 1.2 collective-permute-done
  235.4 2.3 collective-permute-start.3
  237.7 1.3 collective-permute-start.2
  239.1 0.5 collective-permute-start.1
  239.6 1.4 collective-permute-done.3
  241.0 2.8 %collective-permute-done.2 = f32[128,128]{1,0:T(8,128)S(1)} collective-permute-done((f32[128,128]{1,0:T(8,128)S(1)}, f32[128,128]{1,0:T(8,128)S(1)}, u32[]{:S(2)}, u32[]{:S(2)}) %collective-permute-start.2) | collective-permute-done | bytes 65568 | tf_op jit(solution)/shard_map/ppermute | solution.py:356
  243.8 0.0 collective-permute-done.1
  243.8 2.5 collective-permute-start.6
  246.4 1.1 collective-permute-start.5
  247.5 0.5 collective-permute-start.4
  248.0 2.1 collective-permute-done.6
  250.1 2.1 collective-permute-done.5
  252.2 0.0 collective-permute-done.4
  252.2 1.6 collective-permute-start.9
  253.8 1.6 collective-permute-start.8
  255.4 1.0 collective-permute-start.7
  256.4 1.4 collective-permute-done.9
  257.7 1.8 collective-permute-done.8
  259.6 0.1 collective-permute-done.7
  259.7 8.0 %power.1 = f32[1,1536]{1,0:T(1,128)} custom-call(f32[128,128]{1,0:T(8,128)S(1)} %add_add_fusion.refs_0_, f32[128,1536]{1,0:T(8,128)S(1)} %get-tuple-element.16.refs_1_), custom_call_target="tpu_custom_call" | custom-call | tf_op jit(solution)/shard_map/power/pallas_call | solution.py:345
  (6 shorter events, 0.1 us)
Async XLA Ops:
  166.5 9.4 %copy-start = (s32[2,1,128,2,1536]{4,3,2,1,0:T(2,128)S(1)}, s32[2,1,128,2,1536]{4,3,2,1,0:T(2,128)}, u32[]{:S(2)}) copy-start(s32[2,1,128,2,1536]{4,3,2,1,0:T(2,128)} %param.10) | copy-start | bytes 9437188
  166.5 57.1 %all-to-all-start.1 = ((bf16[128,1,128,128]{3,2,1,0:T(8,128)(2,1)}), bf16[128,1,128,128]{3,2,1,0:T(8,128)(2,1)}, u32[]{:S(2)}, u32[]{:S(2)}) async-start(bf16[128,1,128,128]{3,2,1,0:T(8,128)(2,1)} %get-tuple-element.13), calls=%async_computation.1 | async-start | bytes 8388608 | tf_op jit(solution)/shard_map/all_to_all | solution.py:373
  208.3 0.9 copy-start.1
  223.6 1.1 copy-start.2
  234.1 1.3 collective-permute-start
  235.4 5.6 %collective-permute-start.3 = (f32[128,128]{1,0:T(8,128)S(1)}, f32[128,128]{1,0:T(8,128)S(1)}, u32[]{:S(2)}, u32[]{:S(2)}) collective-permute-start(f32[128,128]{1,0:T(8,128)S(1)} %add.51), channel_id=1, source_target_pairs={{0,96},{16,112},{32,64},{48,80},{64,32},{80,48},{96,0},{112,16},{1... | collective-permute-start | bytes 196616 | tf_op jit(solution)/shard_map/ppermute | solution.py:356
  237.7 6.1 %collective-permute-start.2 = (f32[128,128]{1,0:T(8,128)S(1)}, f32[128,128]{1,0:T(8,128)S(1)}, u32[]{:S(2)}, u32[]{:S(2)}) collective-permute-start(f32[128,128]{1,0:T(8,128)S(1)} %add.51), channel_id=1, source_target_pairs={{0,64},{16,80},{32,96},{48,112},{64,0},{80,16},{96,32},{112,48},{1... | collective-permute-start | bytes 196616 | tf_op jit(solution)/shard_map/ppermute | solution.py:356
  239.1 4.7 %collective-permute-start.1 = (f32[128,128]{1,0:T(8,128)S(1)}, f32[128,128]{1,0:T(8,128)S(1)}, u32[]{:S(2)}, u32[]{:S(2)}) collective-permute-start(f32[128,128]{1,0:T(8,128)S(1)} %add.51), channel_id=1, source_target_pairs={{0,32},{16,48},{32,0},{48,16},{64,96},{80,112},{96,64},{112,80},{1... | collective-permute-start | bytes 196616 | tf_op jit(solution)/shard_map/ppermute | solution.py:356
  243.8 6.3 %collective-permute-start.6 = (f32[128,128]{1,0:T(8,128)S(1)}, f32[128,128]{1,0:T(8,128)S(1)}, u32[]{:S(2)}, u32[]{:S(2)}) collective-permute-start(f32[128,128]{1,0:T(8,128)S(1)} %add_add_fusion.2), channel_id=1, source_target_pairs={{0,3},{1,2},{2,1},{3,0},{4,7},{5,6},{6,5},{7,4},{8,11},{9,10},{10,... | collective-permute-start | bytes 196616 | tf_op jit(solution)/shard_map/ppermute | solution.py:356
  246.4 5.8 %collective-permute-start.5 = (f32[128,128]{1,0:T(8,128)S(1)}, f32[128,128]{1,0:T(8,128)S(1)}, u32[]{:S(2)}, u32[]{:S(2)}) collective-permute-start(f32[128,128]{1,0:T(8,128)S(1)} %add_add_fusion.2), channel_id=1, source_target_pairs={{0,2},{1,3},{2,0},{3,1},{4,6},{5,7},{6,4},{7,5},{8,10},{9,11},{10,... | collective-permute-start | bytes 196616 | tf_op jit(solution)/shard_map/ppermute | solution.py:356
  247.5 4.7 %collective-permute-start.4 = (f32[128,128]{1,0:T(8,128)S(1)}, f32[128,128]{1,0:T(8,128)S(1)}, u32[]{:S(2)}, u32[]{:S(2)}) collective-permute-start(f32[128,128]{1,0:T(8,128)S(1)} %add_add_fusion.2), channel_id=1, source_target_pairs={{0,1},{1,0},{2,3},{3,2},{4,5},{5,4},{6,7},{7,6},{8,9},{9,8},{10,11... | collective-permute-start | bytes 196616 | tf_op jit(solution)/shard_map/ppermute | solution.py:356
  252.2 5.6 %collective-permute-start.9 = (f32[128,128]{1,0:T(8,128)S(1)}, f32[128,128]{1,0:T(8,128)S(1)}, u32[]{:S(2)}, u32[]{:S(2)}) collective-permute-start(f32[128,128]{1,0:T(8,128)S(1)} %add_add_fusion.1), channel_id=1, source_target_pairs={{0,12},{1,13},{2,14},{3,15},{4,8},{5,9},{6,10},{7,11},{8,4},{9,5},... | collective-permute-start | bytes 196616 | tf_op jit(solution)/shard_map/ppermute | solution.py:356
  253.8 5.8 %collective-permute-start.8 = (f32[128,128]{1,0:T(8,128)S(1)}, f32[128,128]{1,0:T(8,128)S(1)}, u32[]{:S(2)}, u32[]{:S(2)}) collective-permute-start(f32[128,128]{1,0:T(8,128)S(1)} %add_add_fusion.1), channel_id=1, source_target_pairs={{0,8},{1,9},{2,10},{3,11},{4,12},{5,13},{6,14},{7,15},{8,0},{9,1},... | collective-permute-start | bytes 196616 | tf_op jit(solution)/shard_map/ppermute | solution.py:356
  255.4 4.3 %collective-permute-start.7 = (f32[128,128]{1,0:T(8,128)S(1)}, f32[128,128]{1,0:T(8,128)S(1)}, u32[]{:S(2)}, u32[]{:S(2)}) collective-permute-start(f32[128,128]{1,0:T(8,128)S(1)} %add_add_fusion.1), channel_id=1, source_target_pairs={{0,4},{1,5},{2,6},{3,7},{4,0},{5,1},{6,2},{7,3},{8,12},{9,13},{10,... | collective-permute-start | bytes 196616 | tf_op jit(solution)/shard_map/ppermute | solution.py:356

commit v4 on v3

--- a/solution.py
+++ b/solution.py
@@ -176,7 +176,7 @@
             out_specs=pl.BlockSpec((128, voxels), lambda i, *_: (0, 0)),
         ),
         out_shape=jax.ShapeDtypeStruct((128, voxels), F32),
-        compiler_params=pltpu.CompilerParams(vmem_limit_bytes=48 * 2**20),
+        compiler_params=pltpu.CompilerParams(vmem_limit_bytes=62_000_000),
         cost_estimate=pl.CostEstimate(
             flops=2 * 128 * voxels * 128 * blocks * units,
             bytes_accessed=blocks * units * (128 * 256 + 8 * voxels),
@@ -186,80 +186,86 @@
     )(swap, lags, windows)
 
 
-def second_beam_kernel(list_ref, gain_ref, lag_ref, *refs):
-    window_refs = refs[:LIST_GROUP]
-    before_hbm, out_ref, gram_ref, before_ref, sem = refs[LIST_GROUP:]
-    step = pl.program_id(0)
+def second_beam_kernel(
+    list_ref, gain_ref, lag_ref, before_hbm, windows_hbm, out_ref, gram_ref, before_ref, held_ref, before_sem, sems
+):
     ((place, plane),) = SECOND
-    fetch = pltpu.make_async_copy(before_hbm, before_ref, sem)
-
-    @pl.when(step == 0)
-    def _():
-        fetch.start()
-        out_ref[...] = jnp.zeros_like(out_ref)
-
-    @pl.when(step * LIST_GROUP < list_ref[lag_ref.shape[1]])
-    def _():
+    count = list_ref[lag_ref.shape[1]]
+    groups = (count + LIST_GROUP - 1) // LIST_GROUP
+
+    def fetches(group, half):
+        return [
+            pltpu.make_async_copy(
+                windows_hbm.at[list_ref[group * LIST_GROUP + j], 0], held_ref.at[half, j], sems.at[half, j]
+            )
+            for j in range(LIST_GROUP)
+        ]
+
+    @pl.when(groups > 0)
+    def _():
+        for copy in fetches(0, 0):
+            copy.start()
+
+    before = pltpu.make_async_copy(before_hbm, before_ref, before_sem)
+    before.start()
+    out_ref[...] = jnp.zeros_like(out_ref)
+
+    def one_group(group, carry):
+        half = lax.rem(group, 2)
+
+        @pl.when(group + 1 < groups)
+        def _():
+            for copy in fetches(group + 1, 1 - half):
+                copy.start()
+
+        for copy in fetches(group, half):
+            copy.wait()
+
         def piece(j):
-            block = list_ref[step * LIST_GROUP + j]
-            return (lambda: window_refs[j][0, 0]), (lambda voxels: lag_ref[0, block, place : place + 1, voxels])
+            block = list_ref[group * LIST_GROUP + j]
+            return (lambda: held_ref[half, j]), (lambda voxels: lag_ref[plane, block, place : place + 1, voxels])
 
         add_pieces([piece(j) for j in range(LIST_GROUP)], out_ref)
-
-    @pl.when(step == pl.num_programs(0) - 1)
-    def _():
-        fetch.wait()
-        beam = (before_ref[...] + out_ref[...]) * gain_ref[0]
-        out_ref[...] = beam
-        high = beam.astype(BF)
-        rest = beam - high.astype(F32)
-        middle = rest.astype(BF)
-        low = (rest - middle.astype(F32)).astype(BF)
-        dims = (((1,), (1,)), ((), ()))
-        stacked = jnp.concatenate([high, middle], axis=0)
-        main = lax.dot_general(stacked, stacked, dims, preferred_element_type=F32)
-        cross = main[:128, 128:] + lax.dot_general(high, low, dims, preferred_element_type=F32)
-        gram_ref[...] = main[:128, :128] + (cross + cross.T + main[128:, 128:])
+        return carry
+
+    lax.fori_loop(0, groups, one_group, 0)
+
+    before.wait()
+    beam = (before_ref[...] + out_ref[...]) * gain_ref[0]
+    out_ref[...] = beam
+    high = beam.astype(BF)
+    rest = beam - high.astype(F32)
+    middle = rest.astype(BF)
+    low = (rest - middle.astype(F32)).astype(BF)
+    dims = (((1,), (1,)), ((), ()))
+    stacked = jnp.concatenate([high, middle], axis=0)
+    main = lax.dot_general(stacked, stacked, dims, preferred_element_type=F32)
+    cross = main[:128, 128:] + lax.dot_general(high, low, dims, preferred_element_type=F32)
+    gram_ref[...] = main[:128, :128] + (cross + cross.T + main[128:, 128:])
 
 
 def second_beam(order, gain, lags, windows, before):
     planes, blocks, slots, voxels = lags.shape
-    ((place, plane),) = SECOND
-    steps = blocks // LIST_GROUP
-
-    def window_spec(j):
-        def index(i, order):
-            last = jnp.maximum((order[blocks] + LIST_GROUP - 1) // LIST_GROUP - 1, 0)
-            return (order[jnp.minimum(i, last) * LIST_GROUP + j], 0, 0, 0)
-
-        return pl.BlockSpec((1, 1, 128, 128), index)
-
+    smem, vmem = pl.BlockSpec(memory_space=pltpu.SMEM), pl.BlockSpec(memory_space=pltpu.VMEM)
     return pl.pallas_call(
         second_beam_kernel,
-        grid_spec=pltpu.PrefetchScalarGridSpec(
-            num_scalar_prefetch=1,
-            grid=(steps,),
-            in_specs=[
-                pl.BlockSpec(memory_space=pltpu.SMEM),
-                pl.BlockSpec((1, blocks, slots, voxels), lambda i, *_: (plane, 0, 0, 0)),
-            ]
-            + [window_spec(j) for j in range(LIST_GROUP)]
-            + [pl.BlockSpec(memory_space=pl.ANY)],
-            out_specs=[
-                pl.BlockSpec((128, voxels), lambda i, *_: (0, 0)),
-                pl.BlockSpec((128, 128), lambda i, *_: (0, 0)),
-            ],
-            scratch_shapes=[pltpu.VMEM((128, voxels), F32), pltpu.SemaphoreType.DMA],
-        ),
+        in_specs=[smem, smem, vmem] + [pl.BlockSpec(memory_space=pltpu.HBM)] * 2,
+        out_specs=[vmem, vmem],
         out_shape=[jax.ShapeDtypeStruct((128, voxels), F32), jax.ShapeDtypeStruct((128, 128), F32)],
-        compiler_params=pltpu.CompilerParams(vmem_limit_bytes=48 * 2**20),
+        scratch_shapes=[
+            pltpu.VMEM((128, voxels), F32),
+            pltpu.VMEM((2, LIST_GROUP, 128, 128), BF),
+            pltpu.SemaphoreType.DMA,
+            pltpu.SemaphoreType.DMA((2, LIST_GROUP)),
+        ],
+        compiler_params=pltpu.CompilerParams(vmem_limit_bytes=40 * 2**20),
         cost_estimate=pl.CostEstimate(
             flops=2 * 128 * voxels * 128 * blocks,
             bytes_accessed=blocks * (128 * 256 + 8 * voxels),
             transcendentals=0,
         ),
         name="beam",
-    )(order, gain, lags, *([windows] * LIST_GROUP), before)
+    )(order, gain, lags, before, windows)
 
 
 def live_order(seen):

time: 270 us -> 267 us (0.989)
  transfers between devices with their start and end apart: 11 -> 11, of which waited for: 9 -> 10; matrix products, arithmetic and copies ran while one was open for 1% -> 1% of each run, Pallas kernels for 12% -> 13%
where the time goes in v4:
time: 267 us; the launch traced here: 266 us
  blocking collectives  152 us (57%)
  Pallas kernels  64.1 us (24%)
  waiting for transfers between devices  25 us (9%)
  starting transfers between devices  20 us (7%)
    all_to_all x1, blocking collectives, shards(): first = lax.all_to_all(first, AXES, split_axis=0, concat_axis=0, tiled=True)  152 us
    pallas_call x1, Pallas kernels, first_beam(): pl.pallas_call(kernel, grid_spec=pltpu.PrefetchScalarGridSpec(num_scalar_...  34.5 us
    pallas_call x1, Pallas kernels, make_windows(): pl.pallas_call(window_kernel, grid=(demod_steps + tiles // TILES_PER_STEP...  14.2 us
    ppermute x10, starting transfers between devices, exchange_sum(): lax.ppermute(x, axis, [(i, i ^ k) for i in range(size)])  13.6 us
    all_to_all x1, waiting for transfers between devices, shards(): lax.all_to_all(second, AXES, split_axis=0, concat_axis=0, tiled=True)  12.7 us
    ppermute x10, waiting for transfers between devices, exchange_sum(): lax.ppermute(x, axis, [(i, i ^ k) for i in range(size)])  12.3 us
    pallas_call x1, Pallas kernels, doppler_power(): pl.pallas_call(kernel, out_shape=jax.ShapeDtypeStruct((1, beam.shape[1]),...  7.97 us
    pallas_call x1, Pallas kernels, second_beam(): pl.pallas_call(second_beam_kernel, in_specs=[smem, smem, vmem] + [pl.Bloc...  7.4 us
  transfers between devices with their start and end apart: 11, of which 10 were waited for; matrix products, arithmetic and copies ran while one was open for 1% of the time, Pallas kernels for 13%

profile of v4, /device:TPU:0, one launch (start us, length us, event | category | flops | bytes accessed | tf_op | source)
XLA Modules:
  0.0 265.9 jit_solution(7794498941169141749)
XLA Ops:
  0.0 14.2 %windows.1 = (bf16[128,3,128,128]{3,2,1,0:T(8,128)(2,1)}, bf16[128,1,128,128]{3,2,1,0:T(8,128)(2,1)}) custom-call(s32[256,128]{1,0:T(8,128)} %bitcast.22, s32[4,128]{1,0:T(4,128)} %bitcast.23, bf16[2,16]{1,0:T(2,128)(2,1)} %taps_ref.1, bf16[8,2,64,2048]{3,2,1,0:T(8,128)(2,1)} %echo_ref.1), custom_call_target="tpu_custom_call" | custom-call | flops 2000000000 | bytes 20971520 | tf_op jit(solution)/shard_map/windows/pallas_call | solution.py:92
  14.2 152.2 %all_to_all.10.refs_2_ = bf16[128,3,128,128]{3,2,1,0:T(8,128)(2,1)} all-to-all(bf16[128,3,128,128]{3,2,1,0:T(8,128)(2,1)} %get-tuple-element.11), channel_id=1, replica_groups=mesh['elem'=8,'vox'=16] {'elem','vox'}, dimensions={0} | all-to-all | bytes 25165824 | tf_op jit(solution)/shard_map/all_to_all | solution.py:378
  166.4 6.4 %all-to-all-start.1 = ((bf16[128,1,128,128]{3,2,1,0:T(8,128)(2,1)}), bf16[128,1,128,128]{3,2,1,0:T(8,128)(2,1)}, u32[]{:S(2)}, u32[]{:S(2)}) async-start(bf16[128,1,128,128]{3,2,1,0:T(8,128)(2,1)} %get-tuple-element.14), calls=%async_computation.1 | async-start | bytes 8388608 | tf_op jit(solution)/shard_map/all_to_all | solution.py:379
  173.5 0.7 dynamic-slice_bitcast_fusion
  174.2 0.6 bitcast_add_fusion
  174.8 0.2 convert_reduce_fusion
  175.0 0.1 select_reduce_fusion
  175.1 0.7 pad_add_fusion.list_ref
  175.8 0.5 fusion.1.refs_0_
  176.3 0.0 copy-start
  176.3 34.5 %beam.2.before_hbm = f32[128,1536]{1,0:T(8,128)} custom-call(s32[128]{0:T(128)} %fusion.1.refs_0_, s32[2,128,2,1536]{3,2,1,0:T(2,128)} %bitcast.20, bf16[128,3,128,128]{3,2,1,0:T(8,128)(2,1)} %all_to_all.10.refs_2_), custom_call_target="tpu_custom_call" | custom-call | flops 19327352832 | bytes 17301504 | tf_op jit(solution)/shard_map/beam/pallas_call | solution.py:167
  210.8 12.7 %all-to-all-done.1.windows_hbm = bf16[128,1,128,128]{3,2,1,0:T(8,128)(2,1)} async-done(((bf16[128,1,128,128]{3,2,1,0:T(8,128)(2,1)}), bf16[128,1,128,128]{3,2,1,0:T(8,128)(2,1)}, u32[]{:S(2)}, u32[]{:S(2)}) %all-to-all-start.1) | async-done | bytes 4194336 | tf_op jit(solution)/shard_map/all_to_all | solution.py:379
  223.5 0.0 copy-done
  223.5 0.0 copy-start.1
  223.5 1.1 copy-done.1
  224.6 7.4 %beam.3 = (f32[128,1536]{1,0:T(8,128)S(1)}, f32[128,128]{1,0:T(8,128)S(1)}) custom-call(s32[129]{0:T(256)S(1)} %pad_add_fusion.list_ref, f32[1]{0:T(128)S(6)} %copy.7.gain_ref, s32[2,128,2,1536]{3,2,1,0:T(2,128)S(1)} %bitcast.21, f32[128,1536]{1,0:T(8,128)S(1)} %copy-done.1, bf16[128,1,128,128]{3,2,1,0:T(8,128)(2,1)} %all-to-all-done.1.windows_hbm), custom_call_target="tpu_custom_call" | custom-call | flops 6442450944 | bytes 5767168 | tf_op jit(solution)/shard_map/beam/pallas_call | solution.py:250
  232.0 0.4 collective-permute-start
  232.4 1.0 collective-permute-done
  233.4 1.5 collective-permute-start.3
  234.9 1.7 collective-permute-start.2
  236.5 1.0 collective-permute-start.1
  237.5 1.4 collective-permute-done.3
  238.9 1.7 collective-permute-done.2
  240.6 0.5 collective-permute-done.1
  241.1 3.9 %collective-permute-start.6 = (f32[128,128]{1,0:T(8,128)S(1)}, f32[128,128]{1,0:T(8,128)S(1)}, u32[]{:S(2)}, u32[]{:S(2)}) collective-permute-start(f32[128,128]{1,0:T(8,128)S(1)} %add_add_fusion.2), channel_id=1, source_target_pairs={{0,3},{1,2},{2,1},{3,0},{4,7},{5,6},{6,5},{7,4},{8,11},{9,10},{10,... | collective-permute-start | bytes 196616 | tf_op jit(solution)/shard_map/ppermute | solution.py:362
  245.0 0.4 collective-permute-start.5
  245.4 0.6 collective-permute-start.4
  246.0 1.6 collective-permute-done.6
  247.6 3.3 %collective-permute-done.5 = f32[128,128]{1,0:T(8,128)S(1)} collective-permute-done((f32[128,128]{1,0:T(8,128)S(1)}, f32[128,128]{1,0:T(8,128)S(1)}, u32[]{:S(2)}, u32[]{:S(2)}) %collective-permute-start.5) | collective-permute-done | bytes 65568 | tf_op jit(solution)/shard_map/ppermute | solution.py:362
  250.8 0.0 collective-permute-done.4
  250.8 1.0 collective-permute-start.9
  251.8 1.5 collective-permute-start.8
  253.4 1.6 collective-permute-start.7
  255.0 1.4 collective-permute-done.9
  256.4 1.2 collective-permute-done.8
  257.6 0.3 collective-permute-done.7
  258.0 8.0 %power.1 = f32[1,1536]{1,0:T(1,128)} custom-call(f32[128,128]{1,0:T(8,128)S(1)} %add_add_fusion.refs_0_, f32[128,1536]{1,0:T(8,128)S(1)} %get-tuple-element.16.refs_1_), custom_call_target="tpu_custom_call" | custom-call | tf_op jit(solution)/shard_map/power/pallas_call | solution.py:351
  (5 shorter events, 0.1 us)
Async XLA Ops:
  166.4 57.1 %all-to-all-start.1 = ((bf16[128,1,128,128]{3,2,1,0:T(8,128)(2,1)}), bf16[128,1,128,128]{3,2,1,0:T(8,128)(2,1)}, u32[]{:S(2)}, u32[]{:S(2)}) async-start(bf16[128,1,128,128]{3,2,1,0:T(8,128)(2,1)} %get-tuple-element.14), calls=%async_computation.1 | async-start | bytes 8388608 | tf_op jit(solution)/shard_map/all_to_all | solution.py:379
  176.3 47.2 %copy-start = (s32[2,1,128,2,1536]{4,3,2,1,0:T(2,128)S(1)}, s32[2,1,128,2,1536]{4,3,2,1,0:T(2,128)}, u32[]{:S(2)}) copy-start(s32[2,1,128,2,1536]{4,3,2,1,0:T(2,128)} %param.10) | copy-start | bytes 9437188
  223.5 1.1 copy-start.1
  232.0 1.3 collective-permute-start
  233.4 5.6 %collective-permute-start.3 = (f32[128,128]{1,0:T(8,128)S(1)}, f32[128,128]{1,0:T(8,128)S(1)}, u32[]{:S(2)}, u32[]{:S(2)}) collective-permute-start(f32[128,128]{1,0:T(8,128)S(1)} %add.51), channel_id=1, source_target_pairs={{0,96},{16,112},{32,64},{48,80},{64,32},{80,48},{96,0},{112,16},{1... | collective-permute-start | bytes 196616 | tf_op jit(solution)/shard_map/ppermute | solution.py:362
  234.9 5.8 %collective-permute-start.2 = (f32[128,128]{1,0:T(8,128)S(1)}, f32[128,128]{1,0:T(8,128)S(1)}, u32[]{:S(2)}, u32[]{:S(2)}) collective-permute-start(f32[128,128]{1,0:T(8,128)S(1)} %add.51), channel_id=1, source_target_pairs={{0,64},{16,80},{32,96},{48,112},{64,0},{80,16},{96,32},{112,48},{1... | collective-permute-start | bytes 196616 | tf_op jit(solution)/shard_map/ppermute | solution.py:362
  236.5 4.6 %collective-permute-start.1 = (f32[128,128]{1,0:T(8,128)S(1)}, f32[128,128]{1,0:T(8,128)S(1)}, u32[]{:S(2)}, u32[]{:S(2)}) collective-permute-start(f32[128,128]{1,0:T(8,128)S(1)} %add.51), channel_id=1, source_target_pairs={{0,32},{16,48},{32,0},{48,16},{64,96},{80,112},{96,64},{112,80},{1... | collective-permute-start | bytes 196616 | tf_op jit(solution)/shard_map/ppermute | solution.py:362
  241.1 6.4 %collective-permute-start.6 = (f32[128,128]{1,0:T(8,128)S(1)}, f32[128,128]{1,0:T(8,128)S(1)}, u32[]{:S(2)}, u32[]{:S(2)}) collective-permute-start(f32[128,128]{1,0:T(8,128)S(1)} %add_add_fusion.2), channel_id=1, source_target_pairs={{0,3},{1,2},{2,1},{3,0},{4,7},{5,6},{6,5},{7,4},{8,11},{9,10},{10,... | collective-permute-start | bytes 196616 | tf_op jit(solution)/shard_map/ppermute | solution.py:362
  245.0 5.8 %collective-permute-start.5 = (f32[128,128]{1,0:T(8,128)S(1)}, f32[128,128]{1,0:T(8,128)S(1)}, u32[]{:S(2)}, u32[]{:S(2)}) collective-permute-start(f32[128,128]{1,0:T(8,128)S(1)} %add_add_fusion.2), channel_id=1, source_target_pairs={{0,2},{1,3},{2,0},{3,1},{4,6},{5,7},{6,4},{7,5},{8,10},{9,11},{10,... | collective-permute-start | bytes 196616 | tf_op jit(solution)/shard_map/ppermute | solution.py:362
  245.4 5.4 %collective-permute-start.4 = (f32[128,128]{1,0:T(8,128)S(1)}, f32[128,128]{1,0:T(8,128)S(1)}, u32[]{:S(2)}, u32[]{:S(2)}) collective-permute-start(f32[128,128]{1,0:T(8,128)S(1)} %add_add_fusion.2), channel_id=1, source_target_pairs={{0,1},{1,0},{2,3},{3,2},{4,5},{5,4},{6,7},{7,6},{8,9},{9,8},{10,11... | collective-permute-start | bytes 196616 | tf_op jit(solution)/shard_map/ppermute | solution.py:362
  250.8 5.6 %collective-permute-start.9 = (f32[128,128]{1,0:T(8,128)S(1)}, f32[128,128]{1,0:T(8,128)S(1)}, u32[]{:S(2)}, u32[]{:S(2)}) collective-permute-start(f32[128,128]{1,0:T(8,128)S(1)} %add_add_fusion.1), channel_id=1, source_target_pairs={{0,12},{1,13},{2,14},{3,15},{4,8},{5,9},{6,10},{7,11},{8,4},{9,5},... | collective-permute-start | bytes 196616 | tf_op jit(solution)/shard_map/ppermute | solution.py:362
  251.8 5.8 %collective-permute-start.8 = (f32[128,128]{1,0:T(8,128)S(1)}, f32[128,128]{1,0:T(8,128)S(1)}, u32[]{:S(2)}, u32[]{:S(2)}) collective-permute-start(f32[128,128]{1,0:T(8,128)S(1)} %add_add_fusion.1), channel_id=1, source_target_pairs={{0,8},{1,9},{2,10},{3,11},{4,12},{5,13},{6,14},{7,15},{8,0},{9,1},... | collective-permute-start | bytes 196616 | tf_op jit(solution)/shard_map/ppermute | solution.py:362
  253.4 4.6 %collective-permute-start.7 = (f32[128,128]{1,0:T(8,128)S(1)}, f32[128,128]{1,0:T(8,128)S(1)}, u32[]{:S(2)}, u32[]{:S(2)}) collective-permute-start(f32[128,128]{1,0:T(8,128)S(1)} %add_add_fusion.1), channel_id=1, source_target_pairs={{0,4},{1,5},{2,6},{3,7},{4,0},{5,1},{6,2},{7,3},{8,12},{9,13},{10,... | collective-permute-start | bytes 196616 | tf_op jit(solution)/shard_map/ppermute | solution.py:362

commit v5 on v4

--- a/solution.py
+++ b/solution.py
@@ -13,19 +13,21 @@
 FIRST = ((0, 0), (0, 1), (1, 0))
 SECOND = ((1, 1),)
 TILES_PER_STEP = 32
-MEMBERS_PER_STEP = 2
+MEMBERS_PER_STEP = 4
 LIST_GROUP = 8
 
 
 def window_kernel(seen_hbm, start_ref, taps_ref, echo_ref, first_ref, second_ref, base_ref, band_ref, seen_ref, sem):
     step = pl.program_id(0)
-    demod_steps = base_ref.shape[0] // MEMBERS_PER_STEP
-    planes = base_ref.shape[1]
+    planes = echo_ref.shape[1]
+    zeros = base_ref.shape[0] - 2
+    demod_steps = zeros // (4 * planes * MEMBERS_PER_STEP)
     fetch = pltpu.make_async_copy(seen_hbm, seen_ref, sem)
 
     @pl.when(step == 0)
     def _():
         fetch.start()
+        base_ref[zeros:, :, :] = jnp.zeros((2, 128, 128), F32)
         taps = taps_ref[...].astype(F32)
         offset = lax.broadcasted_iota(jnp.int32, (640, 128), 0) - 4 * lax.broadcasted_iota(jnp.int32, (640, 128), 1)
         for c in range(2):
@@ -48,8 +50,9 @@
             for plane in range(planes):
                 for j in range(4):
                     r = 64 * (4 * plane + j)
-                    base_ref[MEMBERS_PER_STEP * step + m, plane, j, 0:64, :] = out[r : r + 64, 0:128]
-                    base_ref[MEMBERS_PER_STEP * step + m, plane, j, 64:128, :] = out[r : r + 64, 128:256]
+                    part = (MEMBERS_PER_STEP * step + m) * (4 * planes) + (4 * plane + j)
+                    base_ref[part, 0:64, :] = out[r : r + 64, 0:128]
+                    base_ref[part, 64:128, :] = out[r : r + 64, 128:256]
 
     @pl.when(step == demod_steps)
     def _():
@@ -71,14 +74,11 @@
                     start = start_ref[plane * 2 + 1, tile]
                     if place == 0:
                         start = jnp.where(keep, start_ref[plane * 2, tile], start)
-                    member = jnp.maximum(seen, 0)
-                    block = start // 128
-                    shift = start - 128 * block
-                    here = base_ref[member, plane, block]
-                    after = base_ref[member, plane, jnp.minimum(block + 1, 3)]
-                    both = jnp.where(lane >= shift, here, after)
-                    out = pltpu.roll(both, (128 - shift) & 127, 1)
-                    ref[i, k] = jnp.where(seen >= 0, out, 0.0).astype(BF)
+                    part = seen * (4 * planes) + (4 * plane + lax.shift_right_logical(start, 7))
+                    part = jnp.where(seen >= 0, part, zeros)
+                    both = jnp.where(lane >= (start & 127), base_ref[part], base_ref[part + 1])
+                    out = pltpu.roll(both, (0 - start) & 127, 1)
+                    ref[i, k] = out.astype(BF)
 
 
 def make_windows(echoes, taps, seen, starts):
@@ -102,7 +102,7 @@
         ],
         out_specs=[pl.BlockSpec((TILES_PER_STEP, len(units), 128, 128), out_map) for units in (FIRST, SECOND)],
         scratch_shapes=[
-            pltpu.VMEM((members, planes, 4, 128, 128), F32),
+            pltpu.VMEM((4 * members * planes + 2, 128, 128), F32),
             pltpu.VMEM((640, 256), BF),
             pltpu.SMEM(seen.shape, jnp.int32),
             pltpu.SemaphoreType.DMA,

time: 267 us -> 266 us (level)
  transfers between devices with their start and end apart: 11 -> 11, of which waited for: 10 -> 9; matrix products, arithmetic and copies ran while one was open for 1% -> 1% of each run, Pallas kernels for 13% -> 13%
where the time goes in v5:
time: 266 us; the launch traced here: 264 us
  blocking collectives  152 us (57%)
  Pallas kernels  61.7 us (23%)
  waiting for transfers between devices  25.7 us (10%)
  starting transfers between devices  19.7 us (7%)
    all_to_all x1, blocking collectives, shards(): first = lax.all_to_all(first, AXES, split_axis=0, concat_axis=0, tiled=True)  152 us
    pallas_call x1, Pallas kernels, first_beam(): pl.pallas_call(kernel, grid_spec=pltpu.PrefetchScalarGridSpec(num_scalar_...  34.5 us
    ppermute x10, starting transfers between devices, exchange_sum(): lax.ppermute(x, axis, [(i, i ^ k) for i in range(size)])  13.3 us
    ppermute x10, waiting for transfers between devices, exchange_sum(): lax.ppermute(x, axis, [(i, i ^ k) for i in range(size)])  13 us
    all_to_all x1, waiting for transfers between devices, shards(): lax.all_to_all(second, AXES, split_axis=0, concat_axis=0, tiled=True)  12.7 us
    pallas_call x1, Pallas kernels, make_windows(): pl.pallas_call(window_kernel, grid=(demod_steps + tiles // TILES_PER_STEP...  12.6 us
    pallas_call x1, Pallas kernels, doppler_power(): pl.pallas_call(kernel, out_shape=jax.ShapeDtypeStruct((1, beam.shape[1]),...  7.97 us
    pallas_call x1, Pallas kernels, second_beam(): pl.pallas_call(second_beam_kernel, in_specs=[smem, smem, vmem] + [pl.Bloc...  6.6 us
  transfers between devices with their start and end apart: 11, of which 9 were waited for; matrix products, arithmetic and copies ran while one was open for 1% of the time, Pallas kernels for 13%

profile of v5, /device:TPU:0, one launch (start us, length us, event | category | flops | bytes accessed | tf_op | source)
XLA Modules:
  0.0 264.0 jit_solution(7235742191968120227)
XLA Ops:
  0.0 12.6 %windows.1 = (bf16[128,3,128,128]{3,2,1,0:T(8,128)(2,1)}, bf16[128,1,128,128]{3,2,1,0:T(8,128)(2,1)}) custom-call(s32[256,128]{1,0:T(8,128)} %bitcast.22, s32[4,128]{1,0:T(4,128)} %bitcast.23, bf16[2,16]{1,0:T(2,128)(2,1)} %taps_ref.1, bf16[8,2,64,2048]{3,2,1,0:T(8,128)(2,1)} %echo_ref.1), custom_call_target="tpu_custom_call" | custom-call | flops 2000000000 | bytes 20971520 | tf_op jit(solution)/shard_map/windows/pallas_call | solution.py:92
  12.6 152.2 %all_to_all.10.refs_2_ = bf16[128,3,128,128]{3,2,1,0:T(8,128)(2,1)} all-to-all(bf16[128,3,128,128]{3,2,1,0:T(8,128)(2,1)} %get-tuple-element.11), channel_id=1, replica_groups=mesh['elem'=8,'vox'=16] {'elem','vox'}, dimensions={0} | all-to-all | bytes 25165824 | tf_op jit(solution)/shard_map/all_to_all | solution.py:378
  164.8 6.4 %all-to-all-start.1 = ((bf16[128,1,128,128]{3,2,1,0:T(8,128)(2,1)}), bf16[128,1,128,128]{3,2,1,0:T(8,128)(2,1)}, u32[]{:S(2)}, u32[]{:S(2)}) async-start(bf16[128,1,128,128]{3,2,1,0:T(8,128)(2,1)} %get-tuple-element.14), calls=%async_computation.1 | async-start | bytes 8388608 | tf_op jit(solution)/shard_map/all_to_all | solution.py:379
  171.9 0.7 dynamic-slice_bitcast_fusion
  172.6 0.6 bitcast_add_fusion
  173.2 0.2 convert_reduce_fusion
  173.4 0.1 select_reduce_fusion
  173.5 0.7 pad_add_fusion.list_ref
  174.2 0.5 fusion.1.refs_0_
  174.7 0.0 copy-start
  174.7 34.5 %beam.2.before_hbm = f32[128,1536]{1,0:T(8,128)} custom-call(s32[128]{0:T(128)} %fusion.1.refs_0_, s32[2,128,2,1536]{3,2,1,0:T(2,128)} %bitcast.20, bf16[128,3,128,128]{3,2,1,0:T(8,128)(2,1)} %all_to_all.10.refs_2_), custom_call_target="tpu_custom_call" | custom-call | flops 19327352832 | bytes 17301504 | tf_op jit(solution)/shard_map/beam/pallas_call | solution.py:167
  209.2 12.7 %all-to-all-done.1.windows_hbm = bf16[128,1,128,128]{3,2,1,0:T(8,128)(2,1)} async-done(((bf16[128,1,128,128]{3,2,1,0:T(8,128)(2,1)}), bf16[128,1,128,128]{3,2,1,0:T(8,128)(2,1)}, u32[]{:S(2)}, u32[]{:S(2)}) %all-to-all-start.1) | async-done | bytes 4194336 | tf_op jit(solution)/shard_map/all_to_all | solution.py:379
  221.9 0.0 copy-done
  221.9 0.0 copy-start.1
  221.9 1.1 copy-done.1
  223.0 6.6 %beam.3 = (f32[128,1536]{1,0:T(8,128)S(1)}, f32[128,128]{1,0:T(8,128)S(1)}) custom-call(s32[129]{0:T(256)S(1)} %pad_add_fusion.list_ref, f32[1]{0:T(128)S(6)} %copy.7.gain_ref, s32[2,128,2,1536]{3,2,1,0:T(2,128)S(1)} %bitcast.21, f32[128,1536]{1,0:T(8,128)S(1)} %copy-done.1, bf16[128,1,128,128]{3,2,1,0:T(8,128)(2,1)} %all-to-all-done.1.windows_hbm), custom_call_target="tpu_custom_call" | custom-call | flops 6442450944 | bytes 5767168 | tf_op jit(solution)/shard_map/beam/pallas_call | solution.py:250
  229.6 0.4 collective-permute-start
  230.0 1.0 collective-permute-done
  231.0 1.8 collective-permute-start.3
  232.7 2.8 %collective-permute-start.2 = (f32[128,128]{1,0:T(8,128)S(1)}, f32[128,128]{1,0:T(8,128)S(1)}, u32[]{:S(2)}, u32[]{:S(2)}) collective-permute-start(f32[128,128]{1,0:T(8,128)S(1)} %add.51), channel_id=1, source_target_pairs={{0,64},{16,80},{32,96},{48,112},{64,0},{80,16},{96,32},{112,48},{1... | collective-permute-start | bytes 196616 | tf_op jit(solution)/shard_map/ppermute | solution.py:362
  235.5 0.0 collective-permute-start.1
  235.5 1.0 collective-permute-done.3
  236.5 2.3 collective-permute-done.2
  238.9 0.9 collective-permute-done.1
  239.8 3.0 %collective-permute-start.6 = (f32[128,128]{1,0:T(8,128)S(1)}, f32[128,128]{1,0:T(8,128)S(1)}, u32[]{:S(2)}, u32[]{:S(2)}) collective-permute-start(f32[128,128]{1,0:T(8,128)S(1)} %add_add_fusion.2), channel_id=1, source_target_pairs={{0,3},{1,2},{2,1},{3,0},{4,7},{5,6},{6,5},{7,4},{8,11},{9,10},{10,... | collective-permute-start | bytes 196616 | tf_op jit(solution)/shard_map/ppermute | solution.py:362
  242.8 0.9 collective-permute-start.5
  243.8 0.2 collective-permute-start.4
  244.0 1.4 collective-permute-done.6
  245.4 3.2 %collective-permute-done.5 = f32[128,128]{1,0:T(8,128)S(1)} collective-permute-done((f32[128,128]{1,0:T(8,128)S(1)}, f32[128,128]{1,0:T(8,128)S(1)}, u32[]{:S(2)}, u32[]{:S(2)}) %collective-permute-start.5) | collective-permute-done | bytes 65568 | tf_op jit(solution)/shard_map/ppermute | solution.py:362
  248.6 0.0 collective-permute-done.4
  248.6 1.6 collective-permute-start.9
  250.2 1.2 collective-permute-start.8
  251.4 1.4 collective-permute-start.7
  252.8 1.4 collective-permute-done.9
  254.2 1.8 collective-permute-done.8
  256.0 0.0 collective-permute-done.7
  256.0 8.0 %power.1 = f32[1,1536]{1,0:T(1,128)} custom-call(f32[128,128]{1,0:T(8,128)S(1)} %add_add_fusion.refs_0_, f32[128,1536]{1,0:T(8,128)S(1)} %get-tuple-element.16.refs_1_), custom_call_target="tpu_custom_call" | custom-call | tf_op jit(solution)/shard_map/power/pallas_call | solution.py:351
  (5 shorter events, 0.1 us)
Async XLA Ops:
  164.8 57.1 %all-to-all-start.1 = ((bf16[128,1,128,128]{3,2,1,0:T(8,128)(2,1)}), bf16[128,1,128,128]{3,2,1,0:T(8,128)(2,1)}, u32[]{:S(2)}, u32[]{:S(2)}) async-start(bf16[128,1,128,128]{3,2,1,0:T(8,128)(2,1)} %get-tuple-element.14), calls=%async_computation.1 | async-start | bytes 8388608 | tf_op jit(solution)/shard_map/all_to_all | solution.py:379
  174.7 47.2 %copy-start = (s32[2,1,128,2,1536]{4,3,2,1,0:T(2,128)S(1)}, s32[2,1,128,2,1536]{4,3,2,1,0:T(2,128)}, u32[]{:S(2)}) copy-start(s32[2,1,128,2,1536]{4,3,2,1,0:T(2,128)} %param.10) | copy-start | bytes 9437188
  221.9 1.1 copy-start.1
  229.6 1.3 collective-permute-start
  231.0 5.6 %collective-permute-start.3 = (f32[128,128]{1,0:T(8,128)S(1)}, f32[128,128]{1,0:T(8,128)S(1)}, u32[]{:S(2)}, u32[]{:S(2)}) collective-permute-start(f32[128,128]{1,0:T(8,128)S(1)} %add.51), channel_id=1, source_target_pairs={{0,96},{16,112},{32,64},{48,80},{64,32},{80,48},{96,0},{112,16},{1... | collective-permute-start | bytes 196616 | tf_op jit(solution)/shard_map/ppermute | solution.py:362
  232.7 6.1 %collective-permute-start.2 = (f32[128,128]{1,0:T(8,128)S(1)}, f32[128,128]{1,0:T(8,128)S(1)}, u32[]{:S(2)}, u32[]{:S(2)}) collective-permute-start(f32[128,128]{1,0:T(8,128)S(1)} %add.51), channel_id=1, source_target_pairs={{0,64},{16,80},{32,96},{48,112},{64,0},{80,16},{96,32},{112,48},{1... | collective-permute-start | bytes 196616 | tf_op jit(solution)/shard_map/ppermute | solution.py:362
  235.5 4.3 %collective-permute-start.1 = (f32[128,128]{1,0:T(8,128)S(1)}, f32[128,128]{1,0:T(8,128)S(1)}, u32[]{:S(2)}, u32[]{:S(2)}) collective-permute-start(f32[128,128]{1,0:T(8,128)S(1)} %add.51), channel_id=1, source_target_pairs={{0,32},{16,48},{32,0},{48,16},{64,96},{80,112},{96,64},{112,80},{1... | collective-permute-start | bytes 196616 | tf_op jit(solution)/shard_map/ppermute | solution.py:362
  239.8 5.6 %collective-permute-start.6 = (f32[128,128]{1,0:T(8,128)S(1)}, f32[128,128]{1,0:T(8,128)S(1)}, u32[]{:S(2)}, u32[]{:S(2)}) collective-permute-start(f32[128,128]{1,0:T(8,128)S(1)} %add_add_fusion.2), channel_id=1, source_target_pairs={{0,3},{1,2},{2,1},{3,0},{4,7},{5,6},{6,5},{7,4},{8,11},{9,10},{10,... | collective-permute-start | bytes 196616 | tf_op jit(solution)/shard_map/ppermute | solution.py:362
  242.8 5.8 %collective-permute-start.5 = (f32[128,128]{1,0:T(8,128)S(1)}, f32[128,128]{1,0:T(8,128)S(1)}, u32[]{:S(2)}, u32[]{:S(2)}) collective-permute-start(f32[128,128]{1,0:T(8,128)S(1)} %add_add_fusion.2), channel_id=1, source_target_pairs={{0,2},{1,3},{2,0},{3,1},{4,6},{5,7},{6,4},{7,5},{8,10},{9,11},{10,... | collective-permute-start | bytes 196616 | tf_op jit(solution)/shard_map/ppermute | solution.py:362
  243.8 4.8 %collective-permute-start.4 = (f32[128,128]{1,0:T(8,128)S(1)}, f32[128,128]{1,0:T(8,128)S(1)}, u32[]{:S(2)}, u32[]{:S(2)}) collective-permute-start(f32[128,128]{1,0:T(8,128)S(1)} %add_add_fusion.2), channel_id=1, source_target_pairs={{0,1},{1,0},{2,3},{3,2},{4,5},{5,4},{6,7},{7,6},{8,9},{9,8},{10,11... | collective-permute-start | bytes 196616 | tf_op jit(solution)/shard_map/ppermute | solution.py:362
  248.6 5.6 %collective-permute-start.9 = (f32[128,128]{1,0:T(8,128)S(1)}, f32[128,128]{1,0:T(8,128)S(1)}, u32[]{:S(2)}, u32[]{:S(2)}) collective-permute-start(f32[128,128]{1,0:T(8,128)S(1)} %add_add_fusion.1), channel_id=1, source_target_pairs={{0,12},{1,13},{2,14},{3,15},{4,8},{5,9},{6,10},{7,11},{8,4},{9,5},... | collective-permute-start | bytes 196616 | tf_op jit(solution)/shard_map/ppermute | solution.py:362
  250.2 5.8 %collective-permute-start.8 = (f32[128,128]{1,0:T(8,128)S(1)}, f32[128,128]{1,0:T(8,128)S(1)}, u32[]{:S(2)}, u32[]{:S(2)}) collective-permute-start(f32[128,128]{1,0:T(8,128)S(1)} %add_add_fusion.1), channel_id=1, source_target_pairs={{0,8},{1,9},{2,10},{3,11},{4,12},{5,13},{6,14},{7,15},{8,0},{9,1},... | collective-permute-start | bytes 196616 | tf_op jit(solution)/shard_map/ppermute | solution.py:362
  251.4 4.6 %collective-permute-start.7 = (f32[128,128]{1,0:T(8,128)S(1)}, f32[128,128]{1,0:T(8,128)S(1)}, u32[]{:S(2)}, u32[]{:S(2)}) collective-permute-start(f32[128,128]{1,0:T(8,128)S(1)} %add_add_fusion.1), channel_id=1, source_target_pairs={{0,4},{1,5},{2,6},{3,7},{4,0},{5,1},{6,2},{7,3},{8,12},{9,13},{10,... | collective-permute-start | bytes 196616 | tf_op jit(solution)/shard_map/ppermute | solution.py:362

commit v6 on v5

--- a/solution.py
+++ b/solution.py
@@ -15,6 +15,7 @@
 TILES_PER_STEP = 32
 MEMBERS_PER_STEP = 4
 LIST_GROUP = 8
+SPREAD = 64
 
 
 def window_kernel(seen_hbm, start_ref, taps_ref, echo_ref, first_ref, second_ref, base_ref, band_ref, seen_ref, sem):
@@ -173,9 +174,9 @@
                 pl.BlockSpec((planes, group, slots, voxels), lambda i, *_: (0, i, 0, 0)),
                 pl.BlockSpec((group, units, 128, 128), lambda i, *_: (i, 0, 0, 0)),
             ],
-            out_specs=pl.BlockSpec((128, voxels), lambda i, *_: (0, 0)),
+            out_specs=pl.BlockSpec((None, 128, voxels), lambda i, *_: (0, 0, 0)),
         ),
-        out_shape=jax.ShapeDtypeStruct((128, voxels), F32),
+        out_shape=jax.ShapeDtypeStruct((SPREAD, 128, voxels), F32),
         compiler_params=pltpu.CompilerParams(vmem_limit_bytes=62_000_000),
         cost_estimate=pl.CostEstimate(
             flops=2 * 128 * voxels * 128 * blocks * units,
@@ -206,7 +207,7 @@
         for copy in fetches(0, 0):
             copy.start()
 
-    before = pltpu.make_async_copy(before_hbm, before_ref, before_sem)
+    before = pltpu.make_async_copy(before_hbm.at[0], before_ref, before_sem)
     before.start()
     out_ref[...] = jnp.zeros_like(out_ref)
 
@@ -233,10 +234,7 @@
     before.wait()
     beam = (before_ref[...] + out_ref[...]) * gain_ref[0]
     out_ref[...] = beam
-    high = beam.astype(BF)
-    rest = beam - high.astype(F32)
-    middle = rest.astype(BF)
-    low = (rest - middle.astype(F32)).astype(BF)
+    high, middle, low = split(beam)
     dims = (((1,), (1,)), ((), ()))
     stacked = jnp.concatenate([high, middle], axis=0)
     main = lax.dot_general(stacked, stacked, dims, preferred_element_type=F32)
@@ -327,20 +325,27 @@
     return a
 
 
+def split(x):
+    high = x.astype(BF)
+    rest = x - high.astype(F32)
+    middle = rest.astype(BF)
+    return high, middle, (rest - middle.astype(F32)).astype(BF)
+
+
 def power_kernel(samples, gram_ref, beam_ref, out_ref):
     n = gram_ref.shape[0]
     gram = gram_ref[...]
     eye = lax.broadcasted_iota(jnp.int32, (n, n), 0) == lax.broadcasted_iota(jnp.int32, (n, n), 1)
     energy = jnp.sum(jnp.where(eye, gram, 0.0), keepdims=True)
     correlation = gram * (n / energy)
-    filter_matrix = damping * invert(correlation + jnp.where(eye, damping, 0.0))
-    filtered = lax.dot_general(
-        filter_matrix,
-        beam_ref[...],
-        (((0,), (0,)), ((), ())),
-        precision=lax.Precision.HIGHEST,
-        preferred_element_type=F32,
-    ) / jnp.sqrt(energy / samples)
+    beam = split(beam_ref[...])
+    filter_matrix = split(damping * invert(correlation + jnp.where(eye, damping, 0.0)))
+    filtered = jnp.zeros(beam_ref.shape, F32)
+    for pair in (((1, 1), (0, 2)), ((2, 0), (1, 0)), ((0, 1), (0, 0))):
+        lhs = jnp.concatenate([filter_matrix[i] for i, j in pair], axis=1)
+        rhs = jnp.concatenate([beam[j] for i, j in pair], axis=0)
+        filtered = filtered + jnp.dot(lhs, rhs, preferred_element_type=F32)
+    filtered = filtered / jnp.sqrt(energy / samples)
     out_ref[...] = jnp.log(jnp.sum(filtered * filtered, axis=0, keepdims=True) / n + 1e-06)
 
 

time: 266 us -> 266 us (level)
  starting transfers between devices: 19.7 us -> 24.1 us
    ppermute x10, starting transfers between devices: 13.3 us -> 17.7 us  [exchange_sum(): lax.ppermute(x, axis, [(i, i ^ k) for i in range(size)])]
where the time goes in v6:
time: 266 us; the launch traced here: 264 us
  blocking collectives  152 us (57%)
  Pallas kernels  60.7 us (23%)
  starting transfers between devices  24.1 us (9%)
  waiting for transfers between devices  23.6 us (9%)
    all_to_all x1, blocking collectives, shards(): first = lax.all_to_all(first, AXES, split_axis=0, concat_axis=0, tiled=True)  152 us
    pallas_call x1, Pallas kernels, first_beam(): pl.pallas_call(kernel, grid_spec=pltpu.PrefetchScalarGridSpec(num_scalar_...  34.5 us
    ppermute x10, starting transfers between devices, exchange_sum(): lax.ppermute(x, axis, [(i, i ^ k) for i in range(size)])  17.7 us
    all_to_all x1, waiting for transfers between devices, shards(): lax.all_to_all(second, AXES, split_axis=0, concat_axis=0, tiled=True)  12.7 us
    pallas_call x1, Pallas kernels, make_windows(): pl.pallas_call(window_kernel, grid=(demod_steps + tiles // TILES_PER_STEP...  12.6 us
    ppermute x10, waiting for transfers between devices, exchange_sum(): lax.ppermute(x, axis, [(i, i ^ k) for i in range(size)])  10.9 us
    pallas_call x1, Pallas kernels, doppler_power(): pl.pallas_call(kernel, out_shape=jax.ShapeDtypeStruct((1, beam.shape[1]),...  6.97 us
    pallas_call x1, Pallas kernels, second_beam(): pl.pallas_call(second_beam_kernel, in_specs=[smem, smem, vmem] + [pl.Bloc...  6.6 us
  transfers between devices with their start and end apart: 11, of which 9 were waited for; matrix products, arithmetic and copies ran while one was open for 1% of the time, Pallas kernels for 13%

profile of v6, /device:TPU:0, one launch (start us, length us, event | category | flops | bytes accessed | tf_op | source)
XLA Modules:
  0.0 264.1 jit_solution(5783639896739803112)
XLA Ops:
  0.0 12.6 %windows.1 = (bf16[128,3,128,128]{3,2,1,0:T(8,128)(2,1)}, bf16[128,1,128,128]{3,2,1,0:T(8,128)(2,1)}) custom-call(s32[256,128]{1,0:T(8,128)} %bitcast.22, s32[4,128]{1,0:T(4,128)} %bitcast.23, bf16[2,16]{1,0:T(2,128)(2,1)} %taps_ref.1, bf16[8,2,64,2048]{3,2,1,0:T(8,128)(2,1)} %echo_ref.1), custom_call_target="tpu_custom_call" | custom-call | flops 2000000000 | bytes 20971520 | tf_op jit(solution)/shard_map/windows/pallas_call | solution.py:93
  12.6 152.2 %all_to_all.10.refs_2_ = bf16[128,3,128,128]{3,2,1,0:T(8,128)(2,1)} all-to-all(bf16[128,3,128,128]{3,2,1,0:T(8,128)(2,1)} %get-tuple-element.11), channel_id=1, replica_groups=mesh['elem'=8,'vox'=16] {'elem','vox'}, dimensions={0} | all-to-all | bytes 25165824 | tf_op jit(solution)/shard_map/all_to_all | solution.py:383
  164.8 6.4 %all-to-all-start.1 = ((bf16[128,1,128,128]{3,2,1,0:T(8,128)(2,1)}), bf16[128,1,128,128]{3,2,1,0:T(8,128)(2,1)}, u32[]{:S(2)}, u32[]{:S(2)}) async-start(bf16[128,1,128,128]{3,2,1,0:T(8,128)(2,1)} %get-tuple-element.14), calls=%async_computation.1 | async-start | bytes 8388608 | tf_op jit(solution)/shard_map/all_to_all | solution.py:384
  171.9 0.7 dynamic-slice_bitcast_fusion
  172.6 0.6 bitcast_add_fusion
  173.2 0.2 convert_reduce_fusion
  173.4 0.1 select_reduce_fusion
  173.5 0.7 pad_add_fusion.list_ref
  174.2 0.5 fusion.1.refs_0_
  174.7 0.0 copy-start
  174.7 34.5 %beam.2.before_hbm = f32[64,128,1536]{2,1,0:T(8,128)} custom-call(s32[128]{0:T(128)} %fusion.1.refs_0_, s32[2,128,2,1536]{3,2,1,0:T(2,128)} %bitcast.20, bf16[128,3,128,128]{3,2,1,0:T(8,128)(2,1)} %all_to_all.10.refs_2_), custom_call_target="tpu_custom_call" | custom-call | flops 19327352832 | bytes 17301504 | tf_op jit(solution)/shard_map/beam/pallas_call | solution.py:168
  209.2 12.7 %all-to-all-done.1.windows_hbm = bf16[128,1,128,128]{3,2,1,0:T(8,128)(2,1)} async-done(((bf16[128,1,128,128]{3,2,1,0:T(8,128)(2,1)}), bf16[128,1,128,128]{3,2,1,0:T(8,128)(2,1)}, u32[]{:S(2)}, u32[]{:S(2)}) %all-to-all-start.1) | async-done | bytes 4194336 | tf_op jit(solution)/shard_map/all_to_all | solution.py:384
  221.9 0.0 copy-done
  221.9 6.6 %beam.3 = (f32[128,1536]{1,0:T(8,128)S(1)}, f32[128,128]{1,0:T(8,128)S(1)}) custom-call(s32[129]{0:T(256)S(1)} %pad_add_fusion.list_ref, f32[1]{0:T(128)S(6)} %copy.7.gain_ref, s32[2,128,2,1536]{3,2,1,0:T(2,128)S(1)} %bitcast.21, f32[64,128,1536]{2,1,0:T(8,128)} %beam.2.before_hbm, bf16[128,1,128,128]{3,2,1,0:T(8,128)(2,1)} %all-to-all-done.1.windows_hbm), custom_call_target="tpu_custom_call" | custom-call | flops 6442450944 | bytes 5767168 | tf_op jit(solution)/shard_map/beam/pallas_call | solution.py:248
  228.5 2.7 %collective-permute-start = (f32[128,128]{1,0:T(8,128)S(1)}, f32[128,128]{1,0:T(8,128)S(1)}, u32[]{:S(2)}, u32[]{:S(2)}) collective-permute-start(f32[128,128]{1,0:T(8,128)S(1)} %get-tuple-element.15), channel_id=1, source_target_pairs={{0,16},{16,0},{32,48},{48,32},{64,80},{80,64},{96,112},{112,96},{1... | collective-permute-start | bytes 196616 | tf_op jit(solution)/shard_map/ppermute | solution.py:367
  231.2 0.9 collective-permute-done
  232.1 0.1 collective-permute-start.1
  232.2 1.4 collective-permute-start.2
  233.6 3.3 %collective-permute-start.3 = (f32[128,128]{1,0:T(8,128)S(1)}, f32[128,128]{1,0:T(8,128)S(1)}, u32[]{:S(2)}, u32[]{:S(2)}) collective-permute-start(f32[128,128]{1,0:T(8,128)S(1)} %add.51), channel_id=1, source_target_pairs={{0,96},{16,112},{32,64},{48,80},{64,32},{80,48},{96,0},{112,16},{1... | collective-permute-start | bytes 196616 | tf_op jit(solution)/shard_map/ppermute | solution.py:367
  236.9 0.2 collective-permute-done.1
  237.1 1.1 collective-permute-done.2
  238.2 1.3 collective-permute-done.3
  239.5 2.7 %collective-permute-start.4 = (f32[128,128]{1,0:T(8,128)S(1)}, f32[128,128]{1,0:T(8,128)S(1)}, u32[]{:S(2)}, u32[]{:S(2)}) collective-permute-start(f32[128,128]{1,0:T(8,128)S(1)} %add_add_fusion.2), channel_id=1, source_target_pairs={{0,1},{1,0},{2,3},{3,2},{4,5},{5,4},{6,7},{7,6},{8,9},{9,8},{10,11... | collective-permute-start | bytes 196616 | tf_op jit(solution)/shard_map/ppermute | solution.py:367
  242.2 2.3 collective-permute-start.5
  244.5 0.5 collective-permute-start.6
  245.0 0.0 collective-permute-done.4
  245.0 3.0 %collective-permute-done.5 = f32[128,128]{1,0:T(8,128)S(1)} collective-permute-done((f32[128,128]{1,0:T(8,128)S(1)}, f32[128,128]{1,0:T(8,128)S(1)}, u32[]{:S(2)}, u32[]{:S(2)}) %collective-permute-start.5) | collective-permute-done | bytes 65568 | tf_op jit(solution)/shard_map/ppermute | solution.py:367
  248.0 2.0 collective-permute-done.6
  250.0 0.7 collective-permute-start.7
  250.7 0.3 collective-permute-start.8
  250.9 3.8 %collective-permute-start.9 = (f32[128,128]{1,0:T(8,128)S(1)}, f32[128,128]{1,0:T(8,128)S(1)}, u32[]{:S(2)}, u32[]{:S(2)}) collective-permute-start(f32[128,128]{1,0:T(8,128)S(1)} %add_add_fusion.1), channel_id=1, source_target_pairs={{0,12},{1,13},{2,14},{3,15},{4,8},{5,9},{6,10},{7,11},{8,4},{9,5},... | collective-permute-start | bytes 196616 | tf_op jit(solution)/shard_map/ppermute | solution.py:367
  254.7 0.0 collective-permute-done.7
  254.7 1.7 collective-permute-done.8
  256.4 0.7 collective-permute-done.9
  257.1 7.0 %power.1 = f32[1,1536]{1,0:T(1,128)} custom-call(f32[128,128]{1,0:T(8,128)S(1)} %add_add_fusion.refs_0_, f32[128,1536]{1,0:T(8,128)S(1)} %get-tuple-element.16.refs_1_), custom_call_target="tpu_custom_call" | custom-call | tf_op jit(solution)/shard_map/power/pallas_call | solution.py:356
  (5 shorter events, 0.1 us)
Async XLA Ops:
  164.8 57.1 %all-to-all-start.1 = ((bf16[128,1,128,128]{3,2,1,0:T(8,128)(2,1)}), bf16[128,1,128,128]{3,2,1,0:T(8,128)(2,1)}, u32[]{:S(2)}, u32[]{:S(2)}) async-start(bf16[128,1,128,128]{3,2,1,0:T(8,128)(2,1)} %get-tuple-element.14), calls=%async_computation.1 | async-start | bytes 8388608 | tf_op jit(solution)/shard_map/all_to_all | solution.py:384
  174.7 47.2 %copy-start = (s32[2,1,128,2,1536]{4,3,2,1,0:T(2,128)S(1)}, s32[2,1,128,2,1536]{4,3,2,1,0:T(2,128)}, u32[]{:S(2)}) copy-start(s32[2,1,128,2,1536]{4,3,2,1,0:T(2,128)} %param.10) | copy-start | bytes 9437188
  228.5 3.6 %collective-permute-start = (f32[128,128]{1,0:T(8,128)S(1)}, f32[128,128]{1,0:T(8,128)S(1)}, u32[]{:S(2)}, u32[]{:S(2)}) collective-permute-start(f32[128,128]{1,0:T(8,128)S(1)} %get-tuple-element.15), channel_id=1, source_target_pairs={{0,16},{16,0},{32,48},{48,32},{64,80},{80,64},{96,112},{112,96},{1... | collective-permute-start | bytes 196616 | tf_op jit(solution)/shard_map/ppermute | solution.py:367
  232.1 5.0 %collective-permute-start.1 = (f32[128,128]{1,0:T(8,128)S(1)}, f32[128,128]{1,0:T(8,128)S(1)}, u32[]{:S(2)}, u32[]{:S(2)}) collective-permute-start(f32[128,128]{1,0:T(8,128)S(1)} %add.51), channel_id=1, source_target_pairs={{0,32},{16,48},{32,0},{48,16},{64,96},{80,112},{96,64},{112,80},{1... | collective-permute-start | bytes 196616 | tf_op jit(solution)/shard_map/ppermute | solution.py:367
  232.2 6.0 %collective-permute-start.2 = (f32[128,128]{1,0:T(8,128)S(1)}, f32[128,128]{1,0:T(8,128)S(1)}, u32[]{:S(2)}, u32[]{:S(2)}) collective-permute-start(f32[128,128]{1,0:T(8,128)S(1)} %add.51), channel_id=1, source_target_pairs={{0,64},{16,80},{32,96},{48,112},{64,0},{80,16},{96,32},{112,48},{1... | collective-permute-start | bytes 196616 | tf_op jit(solution)/shard_map/ppermute | solution.py:367
  233.6 5.9 %collective-permute-start.3 = (f32[128,128]{1,0:T(8,128)S(1)}, f32[128,128]{1,0:T(8,128)S(1)}, u32[]{:S(2)}, u32[]{:S(2)}) collective-permute-start(f32[128,128]{1,0:T(8,128)S(1)} %add.51), channel_id=1, source_target_pairs={{0,96},{16,112},{32,64},{48,80},{64,32},{80,48},{96,0},{112,16},{1... | collective-permute-start | bytes 196616 | tf_op jit(solution)/shard_map/ppermute | solution.py:367
  239.5 5.4 %collective-permute-start.4 = (f32[128,128]{1,0:T(8,128)S(1)}, f32[128,128]{1,0:T(8,128)S(1)}, u32[]{:S(2)}, u32[]{:S(2)}) collective-permute-start(f32[128,128]{1,0:T(8,128)S(1)} %add_add_fusion.2), channel_id=1, source_target_pairs={{0,1},{1,0},{2,3},{3,2},{4,5},{5,4},{6,7},{7,6},{8,9},{9,8},{10,11... | collective-permute-start | bytes 196616 | tf_op jit(solution)/shard_map/ppermute | solution.py:367
  242.2 5.8 %collective-permute-start.5 = (f32[128,128]{1,0:T(8,128)S(1)}, f32[128,128]{1,0:T(8,128)S(1)}, u32[]{:S(2)}, u32[]{:S(2)}) collective-permute-start(f32[128,128]{1,0:T(8,128)S(1)} %add_add_fusion.2), channel_id=1, source_target_pairs={{0,2},{1,3},{2,0},{3,1},{4,6},{5,7},{6,4},{7,5},{8,10},{9,11},{10,... | collective-permute-start | bytes 196616 | tf_op jit(solution)/shard_map/ppermute | solution.py:367
  244.5 5.5 %collective-permute-start.6 = (f32[128,128]{1,0:T(8,128)S(1)}, f32[128,128]{1,0:T(8,128)S(1)}, u32[]{:S(2)}, u32[]{:S(2)}) collective-permute-start(f32[128,128]{1,0:T(8,128)S(1)} %add_add_fusion.2), channel_id=1, source_target_pairs={{0,3},{1,2},{2,1},{3,0},{4,7},{5,6},{6,5},{7,4},{8,11},{9,10},{10,... | collective-permute-start | bytes 196616 | tf_op jit(solution)/shard_map/ppermute | solution.py:367
  250.0 4.8 %collective-permute-start.7 = (f32[128,128]{1,0:T(8,128)S(1)}, f32[128,128]{1,0:T(8,128)S(1)}, u32[]{:S(2)}, u32[]{:S(2)}) collective-permute-start(f32[128,128]{1,0:T(8,128)S(1)} %add_add_fusion.1), channel_id=1, source_target_pairs={{0,4},{1,5},{2,6},{3,7},{4,0},{5,1},{6,2},{7,3},{8,12},{9,13},{10,... | collective-permute-start | bytes 196616 | tf_op jit(solution)/shard_map/ppermute | solution.py:367
  250.7 5.8 %collective-permute-start.8 = (f32[128,128]{1,0:T(8,128)S(1)}, f32[128,128]{1,0:T(8,128)S(1)}, u32[]{:S(2)}, u32[]{:S(2)}) collective-permute-start(f32[128,128]{1,0:T(8,128)S(1)} %add_add_fusion.1), channel_id=1, source_target_pairs={{0,8},{1,9},{2,10},{3,11},{4,12},{5,13},{6,14},{7,15},{8,0},{9,1},... | collective-permute-start | bytes 196616 | tf_op jit(solution)/shard_map/ppermute | solution.py:367
  250.9 6.2 %collective-permute-start.9 = (f32[128,128]{1,0:T(8,128)S(1)}, f32[128,128]{1,0:T(8,128)S(1)}, u32[]{:S(2)}, u32[]{:S(2)}) collective-permute-start(f32[128,128]{1,0:T(8,128)S(1)} %add_add_fusion.1), channel_id=1, source_target_pairs={{0,12},{1,13},{2,14},{3,15},{4,8},{5,9},{6,10},{7,11},{8,4},{9,5},... | collective-permute-start | bytes 196616 | tf_op jit(solution)/shard_map/ppermute | solution.py:367

commit v7 on v6

--- a/solution.py
+++ b/solution.py
@@ -14,7 +14,7 @@
 SECOND = ((1, 1),)
 TILES_PER_STEP = 32
 MEMBERS_PER_STEP = 4
-LIST_GROUP = 8
+LIST_GROUP = 16
 SPREAD = 64
 
 

time: 266 us -> 264 us (level)
  starting transfers between devices: 24.1 us -> 20.8 us
    ppermute x10, starting transfers between devices: 17.7 us -> 14.4 us  [exchange_sum(): lax.ppermute(x, axis, [(i, i ^ k) for i in range(size)])]
where the time goes in v7:
time: 264 us; the launch traced here: 263 us
  blocking collectives  152 us (58%)
  Pallas kernels  62.3 us (24%)
  waiting for transfers between devices  24.4 us (9%)
  starting transfers between devices  20.8 us (8%)
    all_to_all x1, blocking collectives, shards(): first = lax.all_to_all(first, AXES, split_axis=0, concat_axis=0, tiled=True)  152 us
    pallas_call x1, Pallas kernels, first_beam(): pl.pallas_call(kernel, grid_spec=pltpu.PrefetchScalarGridSpec(num_scalar_...  34.5 us
    ppermute x10, starting transfers between devices, exchange_sum(): lax.ppermute(x, axis, [(i, i ^ k) for i in range(size)])  14.4 us
    all_to_all x1, waiting for transfers between devices, shards(): lax.all_to_all(second, AXES, split_axis=0, concat_axis=0, tiled=True)  12.7 us
    pallas_call x1, Pallas kernels, make_windows(): pl.pallas_call(window_kernel, grid=(demod_steps + tiles // TILES_PER_STEP...  12.6 us
    ppermute x10, waiting for transfers between devices, exchange_sum(): lax.ppermute(x, axis, [(i, i ^ k) for i in range(size)])  11.7 us
    pallas_call x1, Pallas kernels, second_beam(): pl.pallas_call(second_beam_kernel, in_specs=[smem, smem, vmem] + [pl.Bloc...  8.21 us
    pallas_call x1, Pallas kernels, doppler_power(): pl.pallas_call(kernel, out_shape=jax.ShapeDtypeStruct((1, beam.shape[1]),...  6.97 us
  transfers between devices with their start and end apart: 11, of which 9 were waited for; matrix products, arithmetic and copies ran while one was open for 1% of the time, Pallas kernels for 13%

profile of v7, /device:TPU:0, one launch (start us, length us, event | category | flops | bytes accessed | tf_op | source)
XLA Modules:
  0.0 263.3 jit_solution(5150550353685327941)
XLA Ops:
  0.0 12.6 %windows.1 = (bf16[128,3,128,128]{3,2,1,0:T(8,128)(2,1)}, bf16[128,1,128,128]{3,2,1,0:T(8,128)(2,1)}) custom-call(s32[256,128]{1,0:T(8,128)} %bitcast.22, s32[4,128]{1,0:T(4,128)} %bitcast.23, bf16[2,16]{1,0:T(2,128)(2,1)} %taps_ref.1, bf16[8,2,64,2048]{3,2,1,0:T(8,128)(2,1)} %echo_ref.1), custom_call_target="tpu_custom_call" | custom-call | flops 2000000000 | bytes 20971520 | tf_op jit(solution)/shard_map/windows/pallas_call | solution.py:93
  12.6 152.2 %all_to_all.10.refs_2_ = bf16[128,3,128,128]{3,2,1,0:T(8,128)(2,1)} all-to-all(bf16[128,3,128,128]{3,2,1,0:T(8,128)(2,1)} %get-tuple-element.11), channel_id=1, replica_groups=mesh['elem'=8,'vox'=16] {'elem','vox'}, dimensions={0} | all-to-all | bytes 25165824 | tf_op jit(solution)/shard_map/all_to_all | solution.py:383
  164.8 6.4 %all-to-all-start.1 = ((bf16[128,1,128,128]{3,2,1,0:T(8,128)(2,1)}), bf16[128,1,128,128]{3,2,1,0:T(8,128)(2,1)}, u32[]{:S(2)}, u32[]{:S(2)}) async-start(bf16[128,1,128,128]{3,2,1,0:T(8,128)(2,1)} %get-tuple-element.14), calls=%async_computation.1 | async-start | bytes 8388608 | tf_op jit(solution)/shard_map/all_to_all | solution.py:384
  171.9 0.7 dynamic-slice_bitcast_fusion
  172.6 0.6 bitcast_add_fusion
  173.2 0.2 convert_reduce_fusion
  173.4 0.1 select_reduce_fusion
  173.5 0.7 pad_add_fusion.list_ref
  174.2 0.5 fusion.1.refs_0_
  174.7 0.0 copy-start
  174.7 34.5 %beam.2.before_hbm = f32[64,128,1536]{2,1,0:T(8,128)} custom-call(s32[128]{0:T(128)} %fusion.1.refs_0_, s32[2,128,2,1536]{3,2,1,0:T(2,128)} %bitcast.20, bf16[128,3,128,128]{3,2,1,0:T(8,128)(2,1)} %all_to_all.10.refs_2_), custom_call_target="tpu_custom_call" | custom-call | flops 19327352832 | bytes 17301504 | tf_op jit(solution)/shard_map/beam/pallas_call | solution.py:168
  209.2 12.7 %all-to-all-done.1.windows_hbm = bf16[128,1,128,128]{3,2,1,0:T(8,128)(2,1)} async-done(((bf16[128,1,128,128]{3,2,1,0:T(8,128)(2,1)}), bf16[128,1,128,128]{3,2,1,0:T(8,128)(2,1)}, u32[]{:S(2)}, u32[]{:S(2)}) %all-to-all-start.1) | async-done | bytes 4194336 | tf_op jit(solution)/shard_map/all_to_all | solution.py:384
  221.9 0.0 copy-done
  221.9 8.2 %beam.3 = (f32[128,1536]{1,0:T(8,128)S(1)}, f32[128,128]{1,0:T(8,128)S(1)}) custom-call(s32[129]{0:T(256)S(1)} %pad_add_fusion.list_ref, f32[1]{0:T(128)S(6)} %copy.7.gain_ref, s32[2,128,2,1536]{3,2,1,0:T(2,128)S(1)} %bitcast.21, f32[64,128,1536]{2,1,0:T(8,128)} %beam.2.before_hbm, bf16[128,1,128,128]{3,2,1,0:T(8,128)(2,1)} %all-to-all-done.1.windows_hbm), custom_call_target="tpu_custom_call" | custom-call | flops 6442450944 | bytes 5767168 | tf_op jit(solution)/shard_map/beam/pallas_call | solution.py:248
  230.1 0.1 collective-permute-start
  230.2 1.2 collective-permute-done
  231.5 0.1 collective-permute-start.1
  231.5 2.5 collective-permute-start.2
  234.1 2.2 collective-permute-start.3
  236.2 0.2 collective-permute-done.1
  236.4 1.3 collective-permute-done.2
  237.7 1.8 collective-permute-done.3
  239.5 0.1 collective-permute-start.4
  239.6 2.8 %collective-permute-start.5 = (f32[128,128]{1,0:T(8,128)S(1)}, f32[128,128]{1,0:T(8,128)S(1)}, u32[]{:S(2)}, u32[]{:S(2)}) collective-permute-start(f32[128,128]{1,0:T(8,128)S(1)} %add_add_fusion.2), channel_id=1, source_target_pairs={{0,2},{1,3},{2,0},{3,1},{4,6},{5,7},{6,4},{7,5},{8,10},{9,11},{10,... | collective-permute-start | bytes 196616 | tf_op jit(solution)/shard_map/ppermute | solution.py:367
  242.4 1.9 collective-permute-start.6
  244.3 0.0 collective-permute-done.4
  244.3 1.2 collective-permute-done.5
  245.5 2.3 collective-permute-done.6
  247.9 0.9 collective-permute-start.7
  248.7 2.1 collective-permute-start.8
  250.8 1.8 collective-permute-start.9
  252.7 0.0 collective-permute-done.7
  252.7 1.8 collective-permute-done.8
  254.5 1.8 collective-permute-done.9
  256.3 7.0 %power.1 = f32[1,1536]{1,0:T(1,128)} custom-call(f32[128,128]{1,0:T(8,128)S(1)} %add_add_fusion.refs_0_, f32[128,1536]{1,0:T(8,128)S(1)} %get-tuple-element.16.refs_1_), custom_call_target="tpu_custom_call" | custom-call | tf_op jit(solution)/shard_map/power/pallas_call | solution.py:356
  (5 shorter events, 0.1 us)
Async XLA Ops:
  164.8 57.1 %all-to-all-start.1 = ((bf16[128,1,128,128]{3,2,1,0:T(8,128)(2,1)}), bf16[128,1,128,128]{3,2,1,0:T(8,128)(2,1)}, u32[]{:S(2)}, u32[]{:S(2)}) async-start(bf16[128,1,128,128]{3,2,1,0:T(8,128)(2,1)} %get-tuple-element.14), calls=%async_computation.1 | async-start | bytes 8388608 | tf_op jit(solution)/shard_map/all_to_all | solution.py:384
  174.7 47.2 %copy-start = (s32[2,1,128,2,1536]{4,3,2,1,0:T(2,128)S(1)}, s32[2,1,128,2,1536]{4,3,2,1,0:T(2,128)}, u32[]{:S(2)}) copy-start(s32[2,1,128,2,1536]{4,3,2,1,0:T(2,128)} %param.10) | copy-start | bytes 9437188
  230.1 1.3 collective-permute-start
  231.5 4.9 %collective-permute-start.1 = (f32[128,128]{1,0:T(8,128)S(1)}, f32[128,128]{1,0:T(8,128)S(1)}, u32[]{:S(2)}, u32[]{:S(2)}) collective-permute-start(f32[128,128]{1,0:T(8,128)S(1)} %add.51), channel_id=1, source_target_pairs={{0,32},{16,48},{32,0},{48,16},{64,96},{80,112},{96,64},{112,80},{1... | collective-permute-start | bytes 196616 | tf_op jit(solution)/shard_map/ppermute | solution.py:367
  231.5 6.2 %collective-permute-start.2 = (f32[128,128]{1,0:T(8,128)S(1)}, f32[128,128]{1,0:T(8,128)S(1)}, u32[]{:S(2)}, u32[]{:S(2)}) collective-permute-start(f32[128,128]{1,0:T(8,128)S(1)} %add.51), channel_id=1, source_target_pairs={{0,64},{16,80},{32,96},{48,112},{64,0},{80,16},{96,32},{112,48},{1... | collective-permute-start | bytes 196616 | tf_op jit(solution)/shard_map/ppermute | solution.py:367
  234.1 5.5 %collective-permute-start.3 = (f32[128,128]{1,0:T(8,128)S(1)}, f32[128,128]{1,0:T(8,128)S(1)}, u32[]{:S(2)}, u32[]{:S(2)}) collective-permute-start(f32[128,128]{1,0:T(8,128)S(1)} %add.51), channel_id=1, source_target_pairs={{0,96},{16,112},{32,64},{48,80},{64,32},{80,48},{96,0},{112,16},{1... | collective-permute-start | bytes 196616 | tf_op jit(solution)/shard_map/ppermute | solution.py:367
  239.5 4.8 %collective-permute-start.4 = (f32[128,128]{1,0:T(8,128)S(1)}, f32[128,128]{1,0:T(8,128)S(1)}, u32[]{:S(2)}, u32[]{:S(2)}) collective-permute-start(f32[128,128]{1,0:T(8,128)S(1)} %add_add_fusion.2), channel_id=1, source_target_pairs={{0,1},{1,0},{2,3},{3,2},{4,5},{5,4},{6,7},{7,6},{8,9},{9,8},{10,11... | collective-permute-start | bytes 196616 | tf_op jit(solution)/shard_map/ppermute | solution.py:367
  239.6 5.9 %collective-permute-start.5 = (f32[128,128]{1,0:T(8,128)S(1)}, f32[128,128]{1,0:T(8,128)S(1)}, u32[]{:S(2)}, u32[]{:S(2)}) collective-permute-start(f32[128,128]{1,0:T(8,128)S(1)} %add_add_fusion.2), channel_id=1, source_target_pairs={{0,2},{1,3},{2,0},{3,1},{4,6},{5,7},{6,4},{7,5},{8,10},{9,11},{10,... | collective-permute-start | bytes 196616 | tf_op jit(solution)/shard_map/ppermute | solution.py:367
  242.4 5.5 %collective-permute-start.6 = (f32[128,128]{1,0:T(8,128)S(1)}, f32[128,128]{1,0:T(8,128)S(1)}, u32[]{:S(2)}, u32[]{:S(2)}) collective-permute-start(f32[128,128]{1,0:T(8,128)S(1)} %add_add_fusion.2), channel_id=1, source_target_pairs={{0,3},{1,2},{2,1},{3,0},{4,7},{5,6},{6,5},{7,4},{8,11},{9,10},{10,... | collective-permute-start | bytes 196616 | tf_op jit(solution)/shard_map/ppermute | solution.py:367
  247.9 4.8 %collective-permute-start.7 = (f32[128,128]{1,0:T(8,128)S(1)}, f32[128,128]{1,0:T(8,128)S(1)}, u32[]{:S(2)}, u32[]{:S(2)}) collective-permute-start(f32[128,128]{1,0:T(8,128)S(1)} %add_add_fusion.1), channel_id=1, source_target_pairs={{0,4},{1,5},{2,6},{3,7},{4,0},{5,1},{6,2},{7,3},{8,12},{9,13},{10,... | collective-permute-start | bytes 196616 | tf_op jit(solution)/shard_map/ppermute | solution.py:367
  248.7 5.8 %collective-permute-start.8 = (f32[128,128]{1,0:T(8,128)S(1)}, f32[128,128]{1,0:T(8,128)S(1)}, u32[]{:S(2)}, u32[]{:S(2)}) collective-permute-start(f32[128,128]{1,0:T(8,128)S(1)} %add_add_fusion.1), channel_id=1, source_target_pairs={{0,8},{1,9},{2,10},{3,11},{4,12},{5,13},{6,14},{7,15},{8,0},{9,1},... | collective-permute-start | bytes 196616 | tf_op jit(solution)/shard_map/ppermute | solution.py:367
  250.8 5.5 %collective-permute-start.9 = (f32[128,128]{1,0:T(8,128)S(1)}, f32[128,128]{1,0:T(8,128)S(1)}, u32[]{:S(2)}, u32[]{:S(2)}) collective-permute-start(f32[128,128]{1,0:T(8,128)S(1)} %add_add_fusion.1), channel_id=1, source_target_pairs={{0,12},{1,13},{2,14},{3,15},{4,8},{5,9},{6,10},{7,11},{8,4},{9,5},... | collective-permute-start | bytes 196616 | tf_op jit(solution)/shard_map/ppermute | solution.py:367
